TPU v7x, 128 devices: a whole 4x4x4 slice. The times are simulated.
128 devices in a mesh: lat: 8 (over y_lo, z), lon: 16 (over y_hi, x, core).
Axes of the slice: x: 4, y: 4 (y_hi: 2, y_lo: 2; y = y_hi * 2 + y_lo), z: 4, core: 2. Of those that a mesh axis runs over, the one named last changes fastest.
Arguments:
- adjoint_field: float32 [128, 256, 4096], P(None, 'lat', 'lon'), may hold values from -6 to 6
- mixing_inverse: float32 [256, 128, 128], P('lat'), as said below
- cloud_top: int32 [256, 4096], P('lat', 'lon'), may hold values from 1 to 128
- conv_frac: float32 [256, 4096], P('lat', 'lon'), may hold values from 0.2 to 0.9
- thickness: float32 [128], replicated, may hold values from 0.3 to 3
- zonal_shift: int32 [128, 256], P(None, 'lat'), may hold values from 0 to 48
- zonal_frac: float32 [128, 256], P(None, 'lat'), may hold values from 0 to 1
- merid_courant: float32 [128, 256, 4096], P(None, 'lat', 'lon'), may hold values from 0.1 to 0.9
- obs_kernel: bfloat16 [262144, 128], P(('lat', 'lon')), may hold values from -6 to 6
- obs_depart: float32 [262144], P(('lat', 'lon')), may hold values from -6 to 6
- obs_dest: int32 [262144], P(('lat', 'lon')), may hold values from 0 to 127, as said below
- obs_col: int32 [262144], P(('lat', 'lon')), may hold values from 0 to 8191
- obs_count: int32 [128], P(('lat', 'lon')), may hold values from 16 to 2048, as said below
Outputs:
- adjoint_out: float32 [128, 256, 4096], P(None, 'lat', 'lon')
Inputs may be any that keep to these rules, and one draw needn't show every extreme that they name: `obs_dest`: live rows of each device are in non-decreasing order of destination, at most 16 of them to one destination; some destination receives exactly 16 live rows from every device. Rows past a device's count carry no sounding. `obs_count`: some device has all its rows live. `mixing_inverse`: entries are positive.
All inputs are finite; a program needn't handle non-finite values.
Results may differ from a plain program's by a relative error of at most 0.00095.
Values may be sent and summed in bfloat16 or wider, within the bound.
A program may use at most 128 MiB of HBM per device.

v0:
```python
import functools

import jax
import jax.numpy as jnp
from jax import lax
from jax.experimental import pallas as pl
from jax.experimental.pallas import tpu as pltpu
from jax.sharding import PartitionSpec as P

MESH = pl.DeviceIdType.MESH
F32 = jnp.float32
BF16 = jnp.bfloat16
I32 = jnp.int32
DMA = pltpu.SemaphoreType.DMA
NLAT, NLON, NDEV = 8, 16, 128
LEV, ROWS, COLS = 128, 32, 256
OBS, CAP = 2048, 16
PACK = 64


def iota(shape, axis):
    return lax.broadcasted_iota(I32, shape, axis)


def exchange_kernel(
    count_ref, kernel_ref, depart_ref, dest_ref, col_ref, rows_out, meta_out,
    send_rows, send_meta, contribution, entered, sems,
):
    lat, lon = lax.axis_index("lat"), lax.axis_index("lon")
    me = lat * NLON + lon
    barrier = pltpu.get_barrier_semaphore()

    def greet(target_of, semaphore, count):
        def body(step, carry):
            pl.semaphore_signal(semaphore, inc=1, device_id=target_of(step), device_id_type=MESH)
            return carry

        lax.fori_loop(1, count, body, 0)

    lon_peer = lambda step: (lat, lax.rem(lon + step, NLON))
    lat_peer = lambda step: (lax.rem(lat + step, NLAT), lon)
    greet(lon_peer, barrier, NLON)
    greet(lat_peer, barrier, NLAT)

    dest = dest_ref[...]
    sub, lane = iota((16, 128), 0), iota((16, 128), 1)
    flat = sub * 128 + lane
    rank = jnp.zeros((16, 128), I32)
    for step in range(1, CAP):
        rolled = pltpu.roll(dest, step, 1)
        before = jnp.where(lane < step, pltpu.roll(rolled, 1, 0), rolled)
        rank = rank + jnp.where((before == dest) & (flat >= step), 1, 0)
    live = flat < count_ref[0]
    slot = jnp.where(live, dest * CAP + rank, -1)
    dest_live = jnp.where(live, dest, -1)
    cells = col_ref[...]
    cell_row = (cells // COLS).astype(F32)
    cell_col = (cells % COLS).astype(F32)

    depart_t = jnp.transpose(depart_ref[...])
    for block in range(16):
        span = pl.ds(block * 128, 128)
        contribution[span, :] = (
            kernel_ref[span, :].astype(F32) * jnp.broadcast_to(depart_t[:, block : block + 1], (128, 128))
        ).astype(BF16)

    pl.semaphore_wait(barrier, NLON + NLAT - 2)
    greet(lat_peer, entered, NLAT)

    big_sub = iota((128, 128), 0)
    mine = (big_sub // CAP) == lax.rem(me, 8)
    meta = jnp.zeros((128, 128), F32)
    nt = (((1,), (1,)), ((), ()))
    for block in range(16):
        owner = jnp.where(dest_live[block : block + 1, :] == big_sub, 1.0, 0.0).astype(BF16)
        place = (rank[block : block + 1, :] == big_sub % CAP) & mine
        row_part = jnp.where(place, cell_row[block : block + 1, :], 0.0).astype(BF16)
        col_part = jnp.where(place, cell_col[block : block + 1, :], 0.0).astype(BF16)
        meta = meta + float(COLS) * lax.dot_general(owner, row_part, nt, preferred_element_type=F32)
        meta = meta + lax.dot_general(owner, col_part, nt, preferred_element_type=F32)
    meta = meta.astype(I32)
    for dst in range(NDEV):
        send_meta[dst, :, :] = meta[dst : dst + 1, :]

    for out_block in range(16):
        total = jnp.zeros((128, 128), F32)
        for block in range(out_block + 1):
            hit = jnp.where(slot[block : block + 1, :] == big_sub + out_block * 128, 1.0, 0.0).astype(BF16)
            total = total + jnp.dot(
                hit, contribution[pl.ds(block * 128, 128), :], preferred_element_type=F32
            )
        send_rows[pl.ds(out_block * 8, 8), :, :] = total.astype(BF16).reshape(8, CAP, LEV)

    pl.semaphore_wait(entered, NLAT - 1)

    def send(step, carry):
        target = lax.rem(me + step, NDEV)
        where = (target // NLON, lax.rem(target, NLON))
        pltpu.make_async_remote_copy(
            send_rows.at[target], rows_out.at[me], sems.at[0], sems.at[1],
            device_id=where, device_id_type=MESH,
        ).start()
        pltpu.make_async_remote_copy(
            send_meta.at[target], meta_out.at[me], sems.at[2], sems.at[3],
            device_id=where, device_id_type=MESH,
        ).start()
        return carry

    lax.fori_loop(1, NDEV, send, 0)
    own_rows = pltpu.make_async_copy(send_rows.at[me], rows_out.at[me], sems.at[4])
    own_meta = pltpu.make_async_copy(send_meta.at[me], meta_out.at[me], sems.at[5])
    own_rows.start()
    own_meta.start()
    own_rows.wait()
    own_meta.wait()
    others = pl.ds(0, NDEV - 1)
    pltpu.make_async_copy(send_rows.at[others], send_rows.at[others], sems.at[0]).wait()
    pltpu.make_async_copy(send_meta.at[others], send_meta.at[others], sems.at[2]).wait()
    pltpu.make_async_copy(rows_out.at[others], rows_out.at[others], sems.at[1]).wait()
    pltpu.make_async_copy(meta_out.at[others], meta_out.at[others], sems.at[3]).wait()


def exchange(obs_count, obs_kernel, obs_depart, obs_dest, obs_col):
    vmem = pl.BlockSpec(memory_space=pltpu.VMEM)
    return pl.pallas_call(
        exchange_kernel,
        out_shape=[
            jax.ShapeDtypeStruct((NDEV, CAP, LEV), BF16),
            jax.ShapeDtypeStruct((NDEV, 1, 128), I32),
        ],
        in_specs=[pl.BlockSpec(memory_space=pltpu.SMEM)] + [vmem] * 4,
        out_specs=[vmem, vmem],
        scratch_shapes=[
            pltpu.VMEM((NDEV, CAP, LEV), BF16),
            pltpu.VMEM((NDEV, 1, 128), I32),
            pltpu.VMEM((OBS, LEV), BF16),
            pltpu.SemaphoreType.REGULAR,
            DMA((6,)),
        ],
        compiler_params=pltpu.CompilerParams(collective_id=0, has_side_effects=True),
        name="exchange",
    )(
        obs_count, obs_kernel, obs_depart.reshape(16, 128),
        obs_dest.reshape(16, 128), obs_col.reshape(16, 128),
    )


def column_kernel(
    rows_ref, meta_ref, field_ref, mixing_ref, top_ref, frac_ref, thick_ref,
    out_ref, halo_ref, rows_t, cols_hot, row_of, thick_full, masked, forced,
):
    step = pl.program_id(0)

    @pl.when(step == 0)
    def _():
        cells = jnp.sum(meta_ref[...].reshape(16, 8, 128), axis=1)
        row_of[...] = jnp.concatenate(
            [(cells[b : b + 1, :] // COLS) for b in range(16)], axis=1
        ).astype(F32)
        columns = jnp.transpose((cells % COLS).astype(F32))
        eye = jnp.where(iota((128, 128), 0) == iota((128, 128), 1), 1.0, 0.0).astype(BF16)
        wide = iota((128, COLS), 1).astype(F32)
        for b in range(16):
            span = pl.ds(b * 128, 128)
            cols_hot[span, :] = jnp.where(
                jnp.broadcast_to(columns[:, b : b + 1], (128, COLS)) == wide, 1.0, 0.0
            ).astype(BF16)
            rows_t[:, span] = lax.dot_general(
                eye, rows_ref[span, :], (((1,), (1,)), ((), ())), preferred_element_type=F32
            ).astype(BF16)
        thick = jnp.transpose(jnp.broadcast_to(thick_ref[...], (128, 128)))
        thick_full[:, 0:128] = thick
        thick_full[:, 128:256] = thick

    base = (step * 8).astype(F32)
    row_ids = row_of[...]
    for r in range(8):
        mask = jnp.where(row_ids == base + float(r), 1.0, 0.0).astype(BF16)
        masked[pl.ds(r * 128, 128), :] = rows_t[...] * mask
    forced[...] = jnp.dot(masked[...], cols_hot[...], preferred_element_type=F32)
    levels = iota((LEV, COLS), 0)
    flat_field = field_ref.reshape(2048, 128)

    def row(r, carry):
        adjoint = jnp.concatenate(
            [flat_field[pl.ds(r, 128, stride=16), :], flat_field[pl.ds(8 + r, 128, stride=16), :]], axis=1
        )
        start = pl.multiple_of(r * 128, 128)
        value = adjoint + forced[pl.ds(start, 128), :]
        matrix = mixing_ref[r]
        v_hi = value.astype(BF16)
        v_lo = (value - v_hi.astype(F32)).astype(BF16)
        m_hi = matrix.astype(BF16)
        m_lo = (matrix - m_hi.astype(F32)).astype(BF16)
        mixed = (
            jnp.dot(m_hi, v_lo, preferred_element_type=F32)
            + jnp.dot(m_lo, v_hi, preferred_element_type=F32)
        ) + jnp.dot(m_hi, v_hi, preferred_element_type=F32)
        cloudy = levels < top_ref[pl.ds(r, 1), :]
        thick = thick_full[...]
        total = jnp.sum(jnp.where(cloudy, mixed, 0.0), axis=0, keepdims=True)
        mass = jnp.sum(jnp.where(cloudy, thick, 0.0), axis=0, keepdims=True)
        fraction = frac_ref[pl.ds(r, 1), :]
        convected = jnp.where(cloudy, mixed + fraction * (thick * (total / mass) - mixed), mixed)
        out_ref[r] = convected
        low = convected[0:64, 0:128]
        high = pltpu.roll(convected[64:128, 0:128], PACK, 1)
        halo_ref[r] = jnp.where(iota((64, 128), 1) < PACK, low, high)
        return carry

    lax.fori_loop(0, 8, row, 0)


def column_step(rows, meta, field, mixing, top, frac, thick):
    whole = lambda *shape: pl.BlockSpec(shape, lambda i: (0,) * len(shape))
    return pl.pallas_call(
        column_kernel,
        grid=(4,),
        out_shape=[
            jax.ShapeDtypeStruct((ROWS, LEV, COLS), F32),
            jax.ShapeDtypeStruct((ROWS, 64, 128), F32),
        ],
        in_specs=[
            whole(OBS, LEV),
            whole(NDEV, 128),
            pl.BlockSpec((LEV, 1, 16, 128), lambda i: (0, i, 0, 0)),
            pl.BlockSpec((8, LEV, LEV), lambda i: (i, 0, 0)),
            pl.BlockSpec((8, COLS), lambda i: (i, 0)),
            pl.BlockSpec((8, COLS), lambda i: (i, 0)),
            whole(1, LEV),
        ],
        out_specs=[
            pl.BlockSpec((8, LEV, COLS), lambda i: (i, 0, 0)),
            pl.BlockSpec((8, 64, 128), lambda i: (i, 0, 0)),
        ],
        scratch_shapes=[
            pltpu.VMEM((LEV, OBS), BF16),
            pltpu.VMEM((OBS, COLS), BF16),
            pltpu.VMEM((1, OBS), F32),
            pltpu.VMEM((LEV, COLS), F32),
            pltpu.VMEM((8 * LEV, OBS), BF16),
            pltpu.VMEM((8 * LEV, COLS), F32),
        ],
        compiler_params=pltpu.CompilerParams(vmem_limit_bytes=56 * 1024 * 1024),
        name="column",
    )(rows, meta, field, mixing, top, frac, thick)


def transport_kernel(
    conv_ref, halo_ref, next_conv_ref, next_halo_ref, next_shift_ref, next_frac_ref, next_courant_ref,
    shift_ref, frac_ref, courant_ref, out_ref, shift_pad, frac_pad, carried,
):
    step = pl.program_id(0)
    lane = iota((LEV, 128), 1)
    tail = jnp.where(iota((LEV, 128), 0) < 64, 0, PACK)

    def zonal(first, second, packed, shift, fraction):
        def pick(offset):
            index = lane + offset
            inside = index < 128
            wrapped = index & 127
            a = jnp.take_along_axis(first, wrapped, axis=1)
            b = jnp.take_along_axis(second, wrapped, axis=1)
            c = jnp.take_along_axis(packed, (wrapped + tail) & 127, axis=1)
            return jnp.where(inside, a, b), jnp.where(inside, b, c)

        left, right = pick(shift)
        left_next, right_next = pick(shift + 1)
        keep = 1.0 - fraction
        return keep * left + fraction * left_next, keep * right + fraction * right_next

    def doubled(packed):
        return jnp.concatenate([packed, packed], axis=0)

    @pl.when(step == 0)
    def _():
        shift_pad[...] = jnp.concatenate([shift_ref[...], jnp.zeros((LEV, 96), I32)], axis=1)
        frac_pad[...] = jnp.concatenate([frac_ref[...], jnp.zeros((LEV, 96), F32)], axis=1)
        last = lax.axis_index("lat") == NLAT - 1
        shift = jnp.transpose(jnp.broadcast_to(next_shift_ref[...], (128, 128)))
        fraction = jnp.transpose(jnp.broadcast_to(next_frac_ref[...], (128, 128)))
        left, right = zonal(
            next_conv_ref[:, 0:128], next_conv_ref[:, 128:256], doubled(next_halo_ref[...]), shift, fraction
        )
        carried[:, 0:128] = jnp.where(last, 0.0, next_courant_ref[:, 0:128] * left)
        carried[:, 128:256] = jnp.where(last, 0.0, next_courant_ref[:, 128:256] * right)

    flat_courant = courant_ref.reshape(2048, 128)
    flat_out = out_ref.reshape(2048, 128)
    first_row = (3 - step) * 8

    def row(back, carry):
        r = 7 - back
        here = jnp.full((LEV, 128), first_row + r, I32)
        shift = jnp.take_along_axis(shift_pad[...], here, axis=1)
        fraction = jnp.take_along_axis(frac_pad[...], here, axis=1)
        parts = zonal(
            conv_ref[r, :, 0:128], conv_ref[r, :, 128:256], doubled(halo_ref[r]), shift, fraction
        )
        for half in range(2):
            at = pl.ds(half * 8 + r, 128, stride=16)
            span = pl.ds(half * 128, 128)
            moved = flat_courant[at, :] * parts[half]
            flat_out[at, :] = parts[half] - moved + carried[:, span]
            carried[:, span] = moved
        return carry

    lax.fori_loop(0, 8, row, 0)


def transport(conv, halo, next_conv, next_halo, next_shift, next_frac, next_courant, shift, frac, courant):
    whole = lambda *shape: pl.BlockSpec(shape, lambda i: (0,) * len(shape))
    blocked = pl.BlockSpec((LEV, 1, 16, 128), lambda i: (0, 3 - i, 0, 0))
    return pl.pallas_call(
        transport_kernel,
        grid=(4,),
        out_shape=jax.ShapeDtypeStruct((LEV, 4, 16, 128), F32),
        in_specs=[
            pl.BlockSpec((8, LEV, COLS), lambda i: (3 - i, 0, 0)),
            pl.BlockSpec((8, 64, 128), lambda i: (3 - i, 0, 0)),
            whole(LEV, COLS),
            whole(64, 128),
            whole(1, LEV),
            whole(1, LEV),
            whole(LEV, COLS),
            whole(LEV, ROWS),
            whole(LEV, ROWS),
            blocked,
        ],
        out_specs=blocked,
        scratch_shapes=[
            pltpu.VMEM((LEV, 128), I32),
            pltpu.VMEM((LEV, 128), F32),
            pltpu.VMEM((LEV, COLS), F32),
        ],
        compiler_params=pltpu.CompilerParams(vmem_limit_bytes=40 * 1024 * 1024),
        name="transport",
    )(conv, halo, next_conv, next_halo, next_shift, next_frac, next_courant, shift, frac, courant)


def tiles(value):
    return value.reshape(LEV, 4, 8, 2, 128).transpose(0, 1, 3, 2, 4).reshape(LEV, 4, 16, 128)


def untiles(value):
    return value.reshape(LEV, 4, 2, 8, 128).transpose(0, 1, 3, 2, 4).reshape(LEV, ROWS, COLS)


def shards(
    adjoint_field, mixing_inverse, cloud_top, conv_frac, thickness, zonal_shift, zonal_frac,
    merid_courant, obs_kernel, obs_depart, obs_dest, obs_col, obs_count,
):
    lat_pairs = [(i + 1, i) for i in range(NLAT - 1)]
    lon_pairs = [((i + 1) % NLON, i) for i in range(NLON)]
    from_lat = lambda value: lax.ppermute(value, "lat", lat_pairs)
    from_lon = lambda value: lax.ppermute(value, "lon", lon_pairs)
    next_courant = from_lat(merid_courant[:, 0, :])
    next_shift = from_lat(zonal_shift[:, 0].reshape(1, LEV))
    next_frac = from_lat(zonal_frac[:, 0].reshape(1, LEV))
    rows, meta = exchange(obs_count, obs_kernel, obs_depart, obs_dest, obs_col)
    conv, edge = column_step(
        rows.reshape(OBS, LEV), meta.reshape(NDEV, 128), tiles(adjoint_field), mixing_inverse,
        cloud_top, conv_frac, thickness.reshape(1, LEV),
    )
    halo = from_lon(edge)
    next_conv = from_lat(conv[0])
    next_halo = from_lat(halo[0])
    out = transport(
        conv, halo, next_conv, next_halo, next_shift, next_frac, next_courant,
        zonal_shift, zonal_frac, tiles(merid_courant),
    )
    return untiles(out)


def solution(mesh):
    split = P(None, "lat", "lon")
    both = P(("lat", "lon"))
    return jax.shard_map(
        shards,
        mesh=mesh,
        in_specs=(
            split, P("lat", None, None), P("lat", "lon"), P("lat", "lon"), P(), P(None, "lat"), P(None, "lat"),
            split, P(("lat", "lon"), None), both, both, both, both,
        ),
        out_specs=split,
        check_vma=False,
    )
```

profile of v0, /device:TPU:15, one launch (start us, length us, event | category | flops | bytes accessed | tf_op | source)
XLA Modules:
  0.0 86.8 jit_solution(15208089716298017437)
XLA Ops:
  0.0 0.0 copy-start.3
  0.0 0.0 copy-start.2
  0.7 19.9 %exchange.1 = (bf16[128,16,128]{2,1,0:T(8,128)(2,1)}, s32[128,1,128]{2,1,0:T(1,128)}) custom-call(s32[1]{0:T(128)S(6)} %copy.20.count_ref, bf16[2048,128]{1,0:T(8,128)(2,1)} %kernel_ref.1, f32[16,128]{1,0:T(8,128)} %bitcast.37, s32[16,128]{1,0:T(8,128)} %bitcast.38, s32[16,128]{1,0:T(8,128)} %bitcast.39), custom_call_target="tpu_custom_call" | custom-call | tf_op jit(solution)/shard_map/exchange/pallas_call | solution.py:125
  20.5 19.1 %column.1 = (f32[32,128,256]{2,1,0:T(8,128)}, f32[32,64,128]{2,1,0:T(8,128)}) custom-call(bf16[2048,128]{1,0:T(8,128)(2,1)} %bitcast.34, s32[128,128]{1,0:T(8,128)} %bitcast.36, f32[128,4,16,128]{3,2,1,0:T(8,128)} %bitcast.33, f32[32,128,128]{2,1,0:T(8,128)} %mixing_ref.1, s32[32,256]{1,0:T(8,128)} %top_ref.1, f32[32,256]{1,0:T(8,128)} %frac_ref.2, ...), custom_call_target="tpu_custom_call" | custom-call | tf_op jit(solution)/shard_map/column/pallas_call | solution.py:216
  39.6 0.6 collective-permute-start
  40.2 0.0 copy-done.3
  40.2 4.5 %collective-permute-start.4 = (f32[1,128]{1,0:T(1,128)S(1)}, f32[1,128]{1,0:T(1,128)S(1)}, u32[]{:S(2)}, u32[]{:S(2)}) collective-permute-start(f32[1,128]{1,0:T(1,128)S(1)} %slice_bitcast_fusion.2), channel_id=1, source_target_pairs={{16,0},{32,16},{48,32},{64,48},{80,64},{96,80},{112,96},{17,1},{33... | collective-permute-start | bytes 1544 | tf_op jit(solution)/shard_map/ppermute | solution.py:355
  44.7 1.3 %slice.19 = f32[128,1,256]{2,1,0:T(1,128)S(1)} slice(f32[128,32,256]{2,1,0:T(8,128)} %param.20), slice={[0:128], [0:1], [0:256]} | slice | bytes 262144 | tf_op jit(solution)/shard_map/slice | solution.py:357
  46.0 2.0 %collective-permute-start.5 = (f32[128,256]{1,0:T(8,128)S(1)}, f32[128,256]{1,0:T(8,128)S(1)}, u32[]{:S(2)}, u32[]{:S(2)}) collective-permute-start(f32[128,256]{1,0:T(8,128)S(1)} %bitcast.35), channel_id=1, source_target_pairs={{16,0},{32,16},{48,32},{64,48},{80,64},{96,80},{112,96},{17,1},{33... | collective-permute-start | bytes 393224 | tf_op jit(solution)/shard_map/ppermute | solution.py:355
  48.0 0.9 %slice_bitcast_fusion = f32[128,256]{1,0:T(8,128)S(1)} fusion(f32[32,128,256]{2,1,0:T(8,128)} %get-tuple-element.11.conv_ref), kind=kLoop, calls=%fused_computation.1 | loop fusion | bytes 262144 | tf_op jit(solution)/shard_map/squeeze | solution.py:366
  48.9 2.7 %collective-permute-start.1 = (f32[128,256]{1,0:T(8,128)S(1)}, f32[128,256]{1,0:T(8,128)S(1)}, u32[]{:S(2)}, u32[]{:S(2)}) collective-permute-start(f32[128,256]{1,0:T(8,128)S(1)} %slice_bitcast_fusion), channel_id=1, source_target_pairs={{16,0},{32,16},{48,32},{64,48},{80,64},{96,80},{112,96},{17,1},{33... | collective-permute-start | bytes 393224 | tf_op jit(solution)/shard_map/ppermute | solution.py:355
  51.6 6.2 %collective-permute-done.halo_ref = f32[32,64,128]{2,1,0:T(8,128)S(1)} collective-permute-done((f32[32,64,128]{2,1,0:T(8,128)}, f32[32,64,128]{2,1,0:T(8,128)S(1)}, u32[]{:S(2)}, u32[]{:S(2)}) %collective-permute-start) | collective-permute-done | bytes 1048608 | tf_op jit(solution)/shard_map/ppermute | solution.py:356
  57.8 4.4 %collective-permute-start.2 = (f32[64,128]{1,0:T(8,128)S(1)}, f32[64,128]{1,0:T(8,128)S(1)}, u32[]{:S(2)}, u32[]{:S(2)}) collective-permute-start(f32[64,128]{1,0:T(8,128)S(1)} %slice_bitcast_fusion.1), channel_id=1, source_target_pairs={{16,0},{32,16},{48,32},{64,48},{80,64},{96,80},{112,96},{17,1},{33... | collective-permute-start | bytes 98312 | tf_op jit(solution)/shard_map/ppermute | solution.py:355
  62.2 0.0 copy-done.2
  62.2 2.1 %collective-permute-start.3 = (s32[1,128]{1,0:T(1,128)S(1)}, s32[1,128]{1,0:T(1,128)S(1)}, u32[]{:S(2)}, u32[]{:S(2)}) collective-permute-start(s32[1,128]{1,0:T(1,128)S(1)} %slice_bitcast_fusion.3), channel_id=1, source_target_pairs={{16,0},{32,16},{48,32},{64,48},{80,64},{96,80},{112,96},{17,1},{33... | collective-permute-start | bytes 1544 | tf_op jit(solution)/shard_map/ppermute | solution.py:355
  64.3 0.1 copy.15.shift_ref
  64.4 0.1 copy.16.frac_ref
  64.5 0.0 collective-permute-done.4.next_frac_ref
  64.5 2.0 %collective-permute-done.3.next_shift_ref = s32[1,128]{1,0:T(1,128)S(1)} collective-permute-done((s32[1,128]{1,0:T(1,128)S(1)}, s32[1,128]{1,0:T(1,128)S(1)}, u32[]{:S(2)}, u32[]{:S(2)}) %collective-permute-start.3) | collective-permute-done | bytes 544 | tf_op jit(solution)/shard_map/ppermute | solution.py:355
  66.5 0.0 collective-permute-done.5.next_courant_ref
  66.5 0.0 collective-permute-done.1.next_conv_ref
  66.5 0.0 collective-permute-done.2.next_halo_ref
  66.5 0.0 copy-start
  66.5 2.2 %copy-done = f32[128,32,256]{2,1,0:T(8,128)S(1)} copy-done((f32[128,32,256]{2,1,0:T(8,128)S(1)}, f32[128,32,256]{2,1,0:T(8,128)}, u32[]{:S(2)}) %copy-start) | copy-done | bytes 4194328
  68.7 0.0 copy-start.1
  68.7 2.2 %copy-done.1 = f32[32,128,256]{2,1,0:T(8,128)S(1)} copy-done((f32[32,128,256]{2,1,0:T(8,128)S(1)}, f32[32,128,256]{2,1,0:T(8,128)}, u32[]{:S(2)}) %copy-start.1) | copy-done | bytes 4194328
  70.9 15.9 %transport.1 = f32[128,4,16,128]{3,2,1,0:T(8,128)} custom-call(f32[32,128,256]{2,1,0:T(8,128)S(1)} %copy-done.1, f32[32,64,128]{2,1,0:T(8,128)S(1)} %collective-permute-done.halo_ref, f32[128,256]{1,0:T(8,128)S(1)} %collective-permute-done.1.next_conv_ref, f32[64,128]{1,0:T(8,128)S(1)} %collective-permute-done.2.next_halo_ref, ...), custom_call_target="tpu_custom_call" | custom-call | tf_op jit(solution)/shard_map/transport/pallas_call | solution.py:314
  (4 shorter events, 0.0 us)
Async XLA Ops:
  0.0 40.2 %copy-start.3 = (f32[128,32]{0,1:T(8,128)S(1)}, f32[128,32]{0,1:T(8,128)}, u32[]{:S(2)}) copy-start(f32[128,32]{0,1:T(8,128)} %param.19) | copy-start | bytes 49156
  0.0 62.2 %copy-start.2 = (s32[128,32]{0,1:T(8,128)S(1)}, s32[128,32]{0,1:T(8,128)}, u32[]{:S(2)}) copy-start(s32[128,32]{0,1:T(8,128)} %param.18) | copy-start | bytes 49156
  39.6 18.1 %collective-permute-start = (f32[32,64,128]{2,1,0:T(8,128)}, f32[32,64,128]{2,1,0:T(8,128)S(1)}, u32[]{:S(2)}, u32[]{:S(2)}) collective-permute-start(f32[32,64,128]{2,1,0:T(8,128)} %get-tuple-element.12), channel_id=1, source_target_pairs={{1,0},{2,1},{3,2},{4,3},{5,4},{6,5},{7,6},{8,7},{9,8},{10,9},{11,1... | collective-permute-start | bytes 3145736 | tf_op jit(solution)/shard_map/ppermute | solution.py:356
  40.2 24.3 %collective-permute-start.4 = (f32[1,128]{1,0:T(1,128)S(1)}, f32[1,128]{1,0:T(1,128)S(1)}, u32[]{:S(2)}, u32[]{:S(2)}) collective-permute-start(f32[1,128]{1,0:T(1,128)S(1)} %slice_bitcast_fusion.2), channel_id=1, source_target_pairs={{16,0},{32,16},{48,32},{64,48},{80,64},{96,80},{112,96},{17,1},{33... | collective-permute-start | bytes 1544 | tf_op jit(solution)/shard_map/ppermute | solution.py:355
  46.0 20.5 %collective-permute-start.5 = (f32[128,256]{1,0:T(8,128)S(1)}, f32[128,256]{1,0:T(8,128)S(1)}, u32[]{:S(2)}, u32[]{:S(2)}) collective-permute-start(f32[128,256]{1,0:T(8,128)S(1)} %bitcast.35), channel_id=1, source_target_pairs={{16,0},{32,16},{48,32},{64,48},{80,64},{96,80},{112,96},{17,1},{33... | collective-permute-start | bytes 393224 | tf_op jit(solution)/shard_map/ppermute | solution.py:355
  48.9 17.6 %collective-permute-start.1 = (f32[128,256]{1,0:T(8,128)S(1)}, f32[128,256]{1,0:T(8,128)S(1)}, u32[]{:S(2)}, u32[]{:S(2)}) collective-permute-start(f32[128,256]{1,0:T(8,128)S(1)} %slice_bitcast_fusion), channel_id=1, source_target_pairs={{16,0},{32,16},{48,32},{64,48},{80,64},{96,80},{112,96},{17,1},{33... | collective-permute-start | bytes 393224 | tf_op jit(solution)/shard_map/ppermute | solution.py:355
  57.8 8.7 %collective-permute-start.2 = (f32[64,128]{1,0:T(8,128)S(1)}, f32[64,128]{1,0:T(8,128)S(1)}, u32[]{:S(2)}, u32[]{:S(2)}) collective-permute-start(f32[64,128]{1,0:T(8,128)S(1)} %slice_bitcast_fusion.1), channel_id=1, source_target_pairs={{16,0},{32,16},{48,32},{64,48},{80,64},{96,80},{112,96},{17,1},{33... | collective-permute-start | bytes 98312 | tf_op jit(solution)/shard_map/ppermute | solution.py:355
  62.2 4.3 %collective-permute-start.3 = (s32[1,128]{1,0:T(1,128)S(1)}, s32[1,128]{1,0:T(1,128)S(1)}, u32[]{:S(2)}, u32[]{:S(2)}) collective-permute-start(s32[1,128]{1,0:T(1,128)S(1)} %slice_bitcast_fusion.3), channel_id=1, source_target_pairs={{16,0},{32,16},{48,32},{64,48},{80,64},{96,80},{112,96},{17,1},{33... | collective-permute-start | bytes 1544 | tf_op jit(solution)/shard_map/ppermute | solution.py:355
  66.5 2.2 %copy-start = (f32[128,32,256]{2,1,0:T(8,128)S(1)}, f32[128,32,256]{2,1,0:T(8,128)}, u32[]{:S(2)}) copy-start(f32[128,32,256]{2,1,0:T(8,128)} %param.20) | copy-start | bytes 12582916
  68.7 2.2 %copy-start.1 = (f32[32,128,256]{2,1,0:T(8,128)S(1)}, f32[32,128,256]{2,1,0:T(8,128)}, u32[]{:S(2)}) copy-start(f32[32,128,256]{2,1,0:T(8,128)} %get-tuple-element.11.conv_ref) | copy-start | bytes 12582916
where the time goes:
time: 87.2 us; the launch traced here: 86.8 us
  Pallas kernels  54.9 us (63%)
  starting transfers between devices  16.2 us (19%)
  waiting for transfers between devices  8.15 us (9%)
  local copies, waits for them, and re-layouts  6.8 us (8%)
    pallas_call x1, Pallas kernels, exchange(): pl.pallas_call(exchange_kernel, out_shape=[jax.ShapeDtypeStruct((NDEV, CA...  19.9 us
    pallas_call x1, Pallas kernels, column_step(): pl.pallas_call(column_kernel, grid=(4,), out_shape=[jax.ShapeDtypeStruct(...  19.1 us
    pallas_call x1, Pallas kernels, transport(): pl.pallas_call(transport_kernel, grid=(4,), out_shape=jax.ShapeDtypeStruc...  15.9 us
    ppermute x5, starting transfers between devices, shards(): from_lat = lambda value: lax.ppermute(value, 'lat', lat_pairs)  15.6 us
    ppermute x1, waiting for transfers between devices, shards(): from_lon = lambda value: lax.ppermute(value, 'lon', lon_pairs)  6.17 us
    unnamed x11, local copies, waits for them, and re-layouts  4.58 us
    ppermute x5, waiting for transfers between devices, shards(): from_lat = lambda value: lax.ppermute(value, 'lat', lat_pairs)  1.99 us
  transfers between devices with their start and end apart: 6, of which 2 were waited for; matrix products, arithmetic and copies ran while one was open for 3% of the time, Pallas kernels for 0%

commit v1 on v0

--- a/solution.py
+++ b/solution.py
@@ -16,6 +16,7 @@
 LEV, ROWS, COLS = 128, 32, 256
 OBS, CAP = 2048, 16
 PACK = 64
+SHIFT_MAX = 48
 
 
 def iota(shape, axis):
@@ -146,13 +147,46 @@
 
 
 def column_kernel(
-    rows_ref, meta_ref, field_ref, mixing_ref, top_ref, frac_ref, thick_ref,
-    out_ref, halo_ref, rows_t, cols_hot, row_of, thick_full, masked, forced,
+    rows_ref, meta_ref, field_ref, mixing_ref, top_ref, frac_ref, thick_ref, courant_ref, shift_ref, zfrac_ref,
+    out_ref, halo_in, next_in, next_halo_in, next_given_in,
+    rows_t, cols_hot, row_of, thick_full, masked, forced, given, first, edge, halo_sems, next_sems,
 ):
     step = pl.program_id(0)
+    lat, lon = lax.axis_index("lat"), lax.axis_index("lon")
+    west = lax.rem(lon + NLON - 1, NLON)
+    east = lax.rem(lon + 1, NLON)
+    north = lax.rem(lat + NLAT - 1, NLAT)
+    has_north, has_south = lat > 0, lat < NLAT - 1
+
+    def halo_copy(block):
+        return pltpu.make_async_remote_copy(
+            edge.at[pl.ds(block * 8, 8)], halo_in.at[pl.ds(block * 8, 8)],
+            halo_sems.at[0, block], halo_sems.at[1, block], device_id=(lat, west), device_id_type=MESH,
+        )
+
+    def next_copy(which):
+        source = (given, first, edge.at[0])[which]
+        target = (next_given_in, next_in, next_halo_in)[which]
+        column = (lon, lon, west)[which]
+        return pltpu.make_async_remote_copy(
+            source, target, next_sems.at[0, which], next_sems.at[1, which],
+            device_id=(north, column), device_id_type=MESH,
+        )
 
     @pl.when(step == 0)
     def _():
+        barrier = pltpu.get_barrier_semaphore()
+        south = lax.rem(lat + 1, NLAT)
+        for target in (
+            (lat, west), (lat, east), (north, lon), (south, lon), (north, west), (south, east)
+        ):
+            pl.semaphore_signal(barrier, inc=1, device_id=target, device_id_type=MESH)
+        flat_courant = courant_ref.reshape(2048, 128)
+        given[:, 0:128] = flat_courant[pl.ds(0, 128, stride=16), :]
+        given[:, 128:256] = flat_courant[pl.ds(8, 128, stride=16), :]
+        first_shift = jnp.broadcast_to(shift_ref[0:1, :].astype(F32), (128, 128))
+        given[:, 256:384] = jnp.transpose(first_shift)
+        given[:, 384:512] = jnp.transpose(jnp.broadcast_to(zfrac_ref[0:1, :], (128, 128)))
         cells = jnp.sum(meta_ref[...].reshape(16, 8, 128), axis=1)
         row_of[...] = jnp.concatenate(
             [(cells[b : b + 1, :] // COLS) for b in range(16)], axis=1
@@ -171,6 +205,11 @@
         thick = jnp.transpose(jnp.broadcast_to(thick_ref[...], (128, 128)))
         thick_full[:, 0:128] = thick
         thick_full[:, 128:256] = thick
+        pl.semaphore_wait(barrier, 6)
+
+        @pl.when(has_north)
+        def _():
+            next_copy(0).start()
 
     base = (step * 8).astype(F32)
     row_ids = row_of[...]
@@ -205,20 +244,46 @@
         out_ref[r] = convected
         low = convected[0:64, 0:128]
         high = pltpu.roll(convected[64:128, 0:128], PACK, 1)
-        halo_ref[r] = jnp.where(iota((64, 128), 1) < PACK, low, high)
+        edge[step * 8 + r] = jnp.where(iota((64, 128), 1) < PACK, low, high)
         return carry
 
     lax.fori_loop(0, 8, row, 0)
-
-
-def column_step(rows, meta, field, mixing, top, frac, thick):
+    halo_copy(step).start()
+
+    @pl.when((step == 0) & has_north)
+    def _():
+        first[...] = out_ref[0]
+        next_copy(1).start()
+        next_copy(2).start()
+
+    @pl.when(step == 3)
+    def _():
+        @pl.when(has_north)
+        def _():
+            for which in range(3):
+                next_copy(which).wait_send()
+
+        @pl.when(has_south)
+        def _():
+            for which in range(3):
+                next_copy(which).wait_recv()
+
+        for block in range(4):
+            halo_copy(block).wait()
+
+
+def column_step(rows, meta, field, mixing, top, frac, thick, courant, shift, zfrac):
     whole = lambda *shape: pl.BlockSpec(shape, lambda i: (0,) * len(shape))
+    anywhere = pl.BlockSpec(memory_space=pl.ANY)
     return pl.pallas_call(
         column_kernel,
         grid=(4,),
         out_shape=[
             jax.ShapeDtypeStruct((ROWS, LEV, COLS), F32),
             jax.ShapeDtypeStruct((ROWS, 64, 128), F32),
+            jax.ShapeDtypeStruct((LEV, COLS), F32),
+            jax.ShapeDtypeStruct((64, 128), F32),
+            jax.ShapeDtypeStruct((LEV, 512), F32),
         ],
         in_specs=[
             whole(OBS, LEV),
@@ -228,11 +293,11 @@
             pl.BlockSpec((8, COLS), lambda i: (i, 0)),
             pl.BlockSpec((8, COLS), lambda i: (i, 0)),
             whole(1, LEV),
-        ],
-        out_specs=[
-            pl.BlockSpec((8, LEV, COLS), lambda i: (i, 0, 0)),
-            pl.BlockSpec((8, 64, 128), lambda i: (i, 0, 0)),
-        ],
+            pl.BlockSpec((LEV, 1, 16, 128), lambda i: (0, 0, 0, 0)),
+            whole(ROWS, LEV),
+            whole(ROWS, LEV),
+        ],
+        out_specs=[pl.BlockSpec((8, LEV, COLS), lambda i: (i, 0, 0))] + [anywhere] * 4,
         scratch_shapes=[
             pltpu.VMEM((LEV, OBS), BF16),
             pltpu.VMEM((OBS, COLS), BF16),
@@ -240,14 +305,21 @@
             pltpu.VMEM((LEV, COLS), F32),
             pltpu.VMEM((8 * LEV, OBS), BF16),
             pltpu.VMEM((8 * LEV, COLS), F32),
-        ],
-        compiler_params=pltpu.CompilerParams(vmem_limit_bytes=56 * 1024 * 1024),
+            pltpu.VMEM((LEV, 512), F32),
+            pltpu.VMEM((LEV, COLS), F32),
+            pltpu.VMEM((ROWS, 64, 128), F32),
+            DMA((2, 4)),
+            DMA((2, 3)),
+        ],
+        compiler_params=pltpu.CompilerParams(
+            vmem_limit_bytes=56 * 1024 * 1024, collective_id=1, has_side_effects=True
+        ),
         name="column",
-    )(rows, meta, field, mixing, top, frac, thick)
+    )(rows, meta, field, mixing, top, frac, thick, courant, shift, zfrac)
 
 
 def transport_kernel(
-    conv_ref, halo_ref, next_conv_ref, next_halo_ref, next_shift_ref, next_frac_ref, next_courant_ref,
+    conv_ref, halo_ref, next_conv_ref, next_halo_ref, next_given_ref,
     shift_ref, frac_ref, courant_ref, out_ref, shift_pad, frac_pad, carried,
 ):
     step = pl.program_id(0)
@@ -274,16 +346,18 @@
 
     @pl.when(step == 0)
     def _():
-        shift_pad[...] = jnp.concatenate([shift_ref[...], jnp.zeros((LEV, 96), I32)], axis=1)
-        frac_pad[...] = jnp.concatenate([frac_ref[...], jnp.zeros((LEV, 96), F32)], axis=1)
+        rest = jnp.zeros((LEV - ROWS, 128), F32)
+        shifts = jnp.concatenate([shift_ref[...].astype(F32), rest], axis=0)
+        shift_pad[...] = jnp.transpose(shifts).astype(I32)
+        frac_pad[...] = jnp.transpose(jnp.concatenate([frac_ref[...], rest], axis=0))
         last = lax.axis_index("lat") == NLAT - 1
-        shift = jnp.transpose(jnp.broadcast_to(next_shift_ref[...], (128, 128)))
-        fraction = jnp.transpose(jnp.broadcast_to(next_frac_ref[...], (128, 128)))
+        shift = jnp.clip(next_given_ref[:, 256:384], 0.0, float(SHIFT_MAX)).astype(I32)
+        fraction = next_given_ref[:, 384:512]
         left, right = zonal(
             next_conv_ref[:, 0:128], next_conv_ref[:, 128:256], doubled(next_halo_ref[...]), shift, fraction
         )
-        carried[:, 0:128] = jnp.where(last, 0.0, next_courant_ref[:, 0:128] * left)
-        carried[:, 128:256] = jnp.where(last, 0.0, next_courant_ref[:, 128:256] * right)
+        carried[:, 0:128] = jnp.where(last, 0.0, next_given_ref[:, 0:128] * left)
+        carried[:, 128:256] = jnp.where(last, 0.0, next_given_ref[:, 128:256] * right)
 
     flat_courant = courant_ref.reshape(2048, 128)
     flat_out = out_ref.reshape(2048, 128)
@@ -308,7 +382,7 @@
     lax.fori_loop(0, 8, row, 0)
 
 
-def transport(conv, halo, next_conv, next_halo, next_shift, next_frac, next_courant, shift, frac, courant):
+def transport(conv, halo, next_conv, next_halo, next_given, shift, frac, courant):
     whole = lambda *shape: pl.BlockSpec(shape, lambda i: (0,) * len(shape))
     blocked = pl.BlockSpec((LEV, 1, 16, 128), lambda i: (0, 3 - i, 0, 0))
     return pl.pallas_call(
@@ -320,11 +394,9 @@
             pl.BlockSpec((8, 64, 128), lambda i: (3 - i, 0, 0)),
             whole(LEV, COLS),
             whole(64, 128),
-            whole(1, LEV),
-            whole(1, LEV),
-            whole(LEV, COLS),
-            whole(LEV, ROWS),
-            whole(LEV, ROWS),
+            whole(LEV, 512),
+            whole(ROWS, LEV),
+            whole(ROWS, LEV),
             blocked,
         ],
         out_specs=blocked,
@@ -333,9 +405,9 @@
             pltpu.VMEM((LEV, 128), F32),
             pltpu.VMEM((LEV, COLS), F32),
         ],
-        compiler_params=pltpu.CompilerParams(vmem_limit_bytes=40 * 1024 * 1024),
+        compiler_params=pltpu.CompilerParams(vmem_limit_bytes=60 * 1024 * 1024),
         name="transport",
-    )(conv, halo, next_conv, next_halo, next_shift, next_frac, next_courant, shift, frac, courant)
+    )(conv, halo, next_conv, next_halo, next_given, shift, frac, courant)
 
 
 def tiles(value):
@@ -350,25 +422,14 @@
     adjoint_field, mixing_inverse, cloud_top, conv_frac, thickness, zonal_shift, zonal_frac,
     merid_courant, obs_kernel, obs_depart, obs_dest, obs_col, obs_count,
 ):
-    lat_pairs = [(i + 1, i) for i in range(NLAT - 1)]
-    lon_pairs = [((i + 1) % NLON, i) for i in range(NLON)]
-    from_lat = lambda value: lax.ppermute(value, "lat", lat_pairs)
-    from_lon = lambda value: lax.ppermute(value, "lon", lon_pairs)
-    next_courant = from_lat(merid_courant[:, 0, :])
-    next_shift = from_lat(zonal_shift[:, 0].reshape(1, LEV))
-    next_frac = from_lat(zonal_frac[:, 0].reshape(1, LEV))
+    courant = tiles(merid_courant)
+    shift, zfrac = zonal_shift.T, zonal_frac.T
     rows, meta = exchange(obs_count, obs_kernel, obs_depart, obs_dest, obs_col)
-    conv, edge = column_step(
+    conv, halo, next_conv, next_halo, next_given = column_step(
         rows.reshape(OBS, LEV), meta.reshape(NDEV, 128), tiles(adjoint_field), mixing_inverse,
-        cloud_top, conv_frac, thickness.reshape(1, LEV),
+        cloud_top, conv_frac, thickness.reshape(1, LEV), courant, shift, zfrac,
     )
-    halo = from_lon(edge)
-    next_conv = from_lat(conv[0])
-    next_halo = from_lat(halo[0])
-    out = transport(
-        conv, halo, next_conv, next_halo, next_shift, next_frac, next_courant,
-        zonal_shift, zonal_frac, tiles(merid_courant),
-    )
+    out = transport(conv, halo, next_conv, next_halo, next_given, shift, zfrac, courant)
     return untiles(out)
 
 

time: 87.2 us -> 68.3 us (0.78)
  starting transfers between devices: 16.2 us -> 0 us
  Pallas kernels: 54.9 us -> 67.3 us
  waiting for transfers between devices: 8.15 us -> 0 us
  local copies, waits for them, and re-layouts: 6.8 us -> 0 us
    ppermute x6 -> x0, starting transfers between devices: 16.2 us -> none  [the longest x5 15.6 us: shards(): from_lat = lambda value: lax.ppermute(value, 'lat', lat_pairs)]
    pallas_call x1, Pallas kernels: 19.1 us -> 30 us  [column_step(): pl.pallas_call(column_kernel, grid=(4,), out_shape=[jax.ShapeDtypeStruct(...]
    ppermute x6 -> x0, waiting for transfers between devices: 8.15 us -> none  [the longest x1 6.17 us: shards(): from_lon = lambda value: lax.ppermute(value, 'lon', lon_pairs)]
    unnamed x11 -> x0, local copies, waits for them, and re-layouts: 4.58 us -> none
    pallas_call x1, Pallas kernels: 15.9 us -> 17.4 us  [transport(): pl.pallas_call(transport_kernel, grid=(4,), out_shape=jax.ShapeDtypeStruc...]
    slice x1 -> x0, local copies, waits for them, and re-layouts: 1.3 us -> none  [shards(): next_courant = from_lat(merid_courant[:, 0, :])]
    squeeze x2 -> x0, local copies, waits for them, and re-layouts: 0.92 us -> none  [the longest x1 0.92 us: shards(): next_conv = from_lat(conv[0])]
  transfers between devices with their start and end apart: 6 -> 0, of which waited for: 2 -> 0; matrix products, arithmetic and copies ran while one was open for 3% -> 0% of each run, Pallas kernels for 0% -> 0%
where the time goes in v1:
time: 68.3 us; the launch traced here: 68 us
  Pallas kernels  67.3 us (99%)
    pallas_call x1, Pallas kernels, column_step(): pl.pallas_call(column_kernel, grid=(4,), out_shape=[jax.ShapeDtypeStruct(...  30 us
    pallas_call x1, Pallas kernels, exchange(): pl.pallas_call(exchange_kernel, out_shape=[jax.ShapeDtypeStruct((NDEV, CA...  19.9 us
    pallas_call x1, Pallas kernels, transport(): pl.pallas_call(transport_kernel, grid=(4,), out_shape=jax.ShapeDtypeStruc...  17.4 us

profile of v1, /device:TPU:15, one launch (start us, length us, event | category | flops | bytes accessed | tf_op | source)
XLA Modules:
  0.0 68.0 jit_solution(5259151770553635972)
XLA Ops:
  0.7 19.9 %exchange.1 = (bf16[128,16,128]{2,1,0:T(8,128)(2,1)}, s32[128,1,128]{2,1,0:T(1,128)}) custom-call(s32[1]{0:T(128)S(6)} %copy.14.count_ref, bf16[2048,128]{1,0:T(8,128)(2,1)} %kernel_ref.1, f32[16,128]{1,0:T(8,128)} %bitcast.32, s32[16,128]{1,0:T(8,128)} %bitcast.33, s32[16,128]{1,0:T(8,128)} %bitcast.34), custom_call_target="tpu_custom_call" | custom-call | tf_op jit(solution)/shard_map/exchange/pallas_call | solution.py:126
  20.5 30.0 %column.1 = (f32[32,128,256]{2,1,0:T(8,128)}, f32[32,64,128]{2,1,0:T(8,128)}, f32[128,256]{1,0:T(8,128)}, f32[64,128]{1,0:T(8,128)}, f32[128,512]{1,0:T(8,128)}) custom-call(bf16[2048,128]{1,0:T(8,128)(2,1)} %bitcast.26, s32[128,128]{1,0:T(8,128)} %bitcast.27, f32[128,4,16,128]{3,2,1,0:T(8,128)} %bitcast.25, f32[32,128,128]{2,1,0:T(8,128)} %mixing_ref.1, ...), custom_call_target="tpu_custom_call" | custom-call | tf_op jit(solution)/shard_map/column/pallas_call | solution.py:278
  50.5 17.4 %transport.1 = f32[128,4,16,128]{3,2,1,0:T(8,128)} custom-call(f32[32,128,256]{2,1,0:T(8,128)} %get-tuple-element.14.conv_ref, f32[32,64,128]{2,1,0:T(8,128)} %get-tuple-element.15.halo_ref, f32[128,256]{1,0:T(8,128)} %get-tuple-element.16.next_conv_ref, f32[64,128]{1,0:T(8,128)} %get-tuple-element.17.next_halo_ref, ...), custom_call_target="tpu_custom_call" | custom-call | tf_op jit(solution)/shard_map/transport/pallas_call | solution.py:388

commit v2 on v1

--- a/solution.py
+++ b/solution.py
@@ -16,7 +16,10 @@
 LEV, ROWS, COLS = 128, 32, 256
 OBS, CAP = 2048, 16
 PACK = 64
-SHIFT_MAX = 48
+PART = 32
+GROUP = 2
+AHEAD = 4
+UNROLL = 4
 
 
 def iota(shape, axis):
@@ -147,9 +150,10 @@
 
 
 def column_kernel(
-    rows_ref, meta_ref, field_ref, mixing_ref, top_ref, frac_ref, thick_ref, courant_ref, shift_ref, zfrac_ref,
+    rows_ref, meta_ref, field_hbm, mixing_ref, top_ref, frac_ref, thick_ref, courant_ref, shift_ref, zfrac_ref,
     out_ref, halo_in, next_in, next_halo_in, next_given_in,
-    rows_t, cols_hot, row_of, thick_full, masked, forced, given, first, edge, halo_sems, next_sems,
+    rows_t, cols_hot, row_of, thick_full, forced, given, first, edge, field, mass, weights, halo_sems, next_sems,
+    field_sems,
 ):
     step = pl.program_id(0)
     lat, lon = lax.axis_index("lat"), lax.axis_index("lon")
@@ -175,6 +179,14 @@
 
     @pl.when(step == 0)
     def _():
+        def fetch(row, carry):
+            for half in range(2):
+                pltpu.make_async_copy(
+                    field_hbm.at[:, place(row, half), :], field.at[row, half], field_sems.at[row // 8]
+                ).start()
+            return carry
+
+        lax.fori_loop(0, ROWS, fetch, 0)
         barrier = pltpu.get_barrier_semaphore()
         south = lax.rem(lat + 1, NLAT)
         for target in (
@@ -182,29 +194,33 @@
         ):
             pl.semaphore_signal(barrier, inc=1, device_id=target, device_id_type=MESH)
         flat_courant = courant_ref.reshape(2048, 128)
-        given[:, 0:128] = flat_courant[pl.ds(0, 128, stride=16), :]
-        given[:, 128:256] = flat_courant[pl.ds(8, 128, stride=16), :]
-        first_shift = jnp.broadcast_to(shift_ref[0:1, :].astype(F32), (128, 128))
-        given[:, 256:384] = jnp.transpose(first_shift)
-        given[:, 384:512] = jnp.transpose(jnp.broadcast_to(zfrac_ref[0:1, :], (128, 128)))
+        given[0:128, 0:128] = flat_courant[pl.ds(0, 128, stride=16), :]
+        given[0:128, 128:256] = flat_courant[pl.ds(8, 128, stride=16), :]
+        given[128:136, 0:128] = shift_ref[0:8, :].astype(F32)
+        given[128:136, 128:256] = jnp.zeros((8, 128), F32)
+        blank = jnp.zeros((LEV - ROWS, 128), F32)
+        weights[...] = jnp.transpose(jnp.concatenate([zfrac_ref[...], blank], axis=0))
         cells = jnp.sum(meta_ref[...].reshape(16, 8, 128), axis=1)
-        row_of[...] = jnp.concatenate(
-            [(cells[b : b + 1, :] // COLS) for b in range(16)], axis=1
-        ).astype(F32)
+        cell_rows = (cells // COLS).astype(F32)
         columns = jnp.transpose((cells % COLS).astype(F32))
         eye = jnp.where(iota((128, 128), 0) == iota((128, 128), 1), 1.0, 0.0).astype(BF16)
         wide = iota((128, COLS), 1).astype(F32)
         for b in range(16):
+            row_of[:, b * 128 : b * 128 + 128] = cell_rows[b : b + 1, :]
             span = pl.ds(b * 128, 128)
             cols_hot[span, :] = jnp.where(
                 jnp.broadcast_to(columns[:, b : b + 1], (128, COLS)) == wide, 1.0, 0.0
             ).astype(BF16)
             rows_t[:, span] = lax.dot_general(
                 eye, rows_ref[span, :], (((1,), (1,)), ((), ())), preferred_element_type=F32
-            ).astype(BF16)
+            )
         thick = jnp.transpose(jnp.broadcast_to(thick_ref[...], (128, 128)))
-        thick_full[:, 0:128] = thick
-        thick_full[:, 128:256] = thick
+        thick_full[...] = thick
+        below = jnp.where(iota((128, 128), 0) <= iota((128, 128), 1), thick, 0.0)
+        sums = jnp.broadcast_to(jnp.sum(below, axis=0, keepdims=True), (ROWS, 128))
+        for half in range(2):
+            span = pl.ds(half * 128, 128)
+            mass[:, span] = jnp.take_along_axis(sums, top_ref[:, span] - 1, axis=1, mode="promise_in_bounds")
         pl.semaphore_wait(barrier, 6)
 
         @pl.when(has_north)
@@ -213,41 +229,51 @@
 
     base = (step * 8).astype(F32)
     row_ids = row_of[...]
-    for r in range(8):
-        mask = jnp.where(row_ids == base + float(r), 1.0, 0.0).astype(BF16)
-        masked[pl.ds(r * 128, 128), :] = rows_t[...] * mask
-    forced[...] = jnp.dot(masked[...], cols_hot[...], preferred_element_type=F32)
-    levels = iota((LEV, COLS), 0)
-    flat_field = field_ref.reshape(2048, 128)
-
-    def row(r, carry):
-        adjoint = jnp.concatenate(
-            [flat_field[pl.ds(r, 128, stride=16), :], flat_field[pl.ds(8 + r, 128, stride=16), :]], axis=1
-        )
-        start = pl.multiple_of(r * 128, 128)
-        value = adjoint + forced[pl.ds(start, 128), :]
+    pieces = [jnp.where(row_ids == base + float(r), rows_t[...], 0.0).astype(BF16) for r in range(8)]
+    forced[...] = jnp.dot(jnp.concatenate(pieces, axis=0), cols_hot[...], preferred_element_type=F32)
+    lane = iota((LEV, 128), 1)
+    low_lane = (lane[0:64, :] < PACK - 1) | (lane[0:64, :] == 127)
+    here = pl.ds(step * 8, 8)
+    pltpu.make_async_copy(field.at[here], field.at[here], field_sems.at[step]).wait()
+    levels = iota((LEV, 128), 0)
+
+    def one_row(r):
+        row = step * 8 + r
+        tops, fractions, masses = (ref[pl.ds(row, 1), :] for ref in (top_ref, frac_ref, mass))
         matrix = mixing_ref[r]
-        v_hi = value.astype(BF16)
-        v_lo = (value - v_hi.astype(F32)).astype(BF16)
         m_hi = matrix.astype(BF16)
         m_lo = (matrix - m_hi.astype(F32)).astype(BF16)
-        mixed = (
-            jnp.dot(m_hi, v_lo, preferred_element_type=F32)
-            + jnp.dot(m_lo, v_hi, preferred_element_type=F32)
-        ) + jnp.dot(m_hi, v_hi, preferred_element_type=F32)
-        cloudy = levels < top_ref[pl.ds(r, 1), :]
-        thick = thick_full[...]
-        total = jnp.sum(jnp.where(cloudy, mixed, 0.0), axis=0, keepdims=True)
-        mass = jnp.sum(jnp.where(cloudy, thick, 0.0), axis=0, keepdims=True)
-        fraction = frac_ref[pl.ds(r, 1), :]
-        convected = jnp.where(cloudy, mixed + fraction * (thick * (total / mass) - mixed), mixed)
-        out_ref[r] = convected
-        low = convected[0:64, 0:128]
-        high = pltpu.roll(convected[64:128, 0:128], PACK, 1)
-        edge[step * 8 + r] = jnp.where(iota((64, 128), 1) < PACK, low, high)
+        left = jnp.concatenate([m_hi, m_lo, m_hi], axis=1)
+        parts = []
+        for half in range(2):
+            span = pl.ds(half * 128, 128)
+            start = pl.multiple_of(r * 128, 128)
+            value = field[row, half] + forced[pl.ds(start, 128), span]
+            v_hi = value.astype(BF16)
+            v_lo = (value - v_hi.astype(F32)).astype(BF16)
+            mixed = jnp.dot(left, jnp.concatenate([v_hi, v_hi, v_lo], axis=0), preferred_element_type=F32)
+            cloudy = levels < tops[:, half * 128 : half * 128 + 128]
+            total = jnp.sum(jnp.where(cloudy, mixed, 0.0), axis=0, keepdims=True)
+            fraction = fractions[:, half * 128 : half * 128 + 128]
+            share = fraction * (total / masses[:, half * 128 : half * 128 + 128])
+            convected = jnp.where(cloudy, mixed * (1.0 - fraction) + thick_full[...] * share, mixed)
+            parts.append(convected)
+        weight = jnp.take_along_axis(
+            weights[...], jnp.full((LEV, 128), row, I32), axis=1, mode="promise_in_bounds"
+        )
+        turned = [pltpu.roll(part, 127, 1) for part in parts]
+        between = parts[0] + weight * (jnp.where(lane == 127, turned[1], turned[0]) - parts[0])
+        out_ref[r, :, 0:128] = between
+        out_ref[r, :, 128:256] = parts[1] + weight * (jnp.where(lane == 127, 0.0, turned[1]) - parts[1])
+        sent = jnp.where(lane == 127, weight * turned[0], between)
+        edge[row] = jnp.where(low_lane, sent[0:64, :], pltpu.roll(sent[64:128, :], PACK, 1)).astype(BF16)
+
+    def rows_of(pair, carry):
+        for i in range(UNROLL):
+            one_row(pair * UNROLL + i)
         return carry
 
-    lax.fori_loop(0, 8, row, 0)
+    lax.fori_loop(0, 8 // UNROLL, rows_of, 0)
     halo_copy(step).start()
 
     @pl.when((step == 0) & has_north)
@@ -280,18 +306,18 @@
         grid=(4,),
         out_shape=[
             jax.ShapeDtypeStruct((ROWS, LEV, COLS), F32),
-            jax.ShapeDtypeStruct((ROWS, 64, 128), F32),
+            jax.ShapeDtypeStruct((ROWS, 64, 128), BF16),
             jax.ShapeDtypeStruct((LEV, COLS), F32),
-            jax.ShapeDtypeStruct((64, 128), F32),
-            jax.ShapeDtypeStruct((LEV, 512), F32),
+            jax.ShapeDtypeStruct((64, 128), BF16),
+            jax.ShapeDtypeStruct((LEV + 8, COLS), F32),
         ],
         in_specs=[
             whole(OBS, LEV),
             whole(NDEV, 128),
-            pl.BlockSpec((LEV, 1, 16, 128), lambda i: (0, i, 0, 0)),
+            anywhere,
             pl.BlockSpec((8, LEV, LEV), lambda i: (i, 0, 0)),
-            pl.BlockSpec((8, COLS), lambda i: (i, 0)),
-            pl.BlockSpec((8, COLS), lambda i: (i, 0)),
+            whole(ROWS, COLS),
+            whole(ROWS, COLS),
             whole(1, LEV),
             pl.BlockSpec((LEV, 1, 16, 128), lambda i: (0, 0, 0, 0)),
             whole(ROWS, LEV),
@@ -299,115 +325,149 @@
         ],
         out_specs=[pl.BlockSpec((8, LEV, COLS), lambda i: (i, 0, 0))] + [anywhere] * 4,
         scratch_shapes=[
-            pltpu.VMEM((LEV, OBS), BF16),
+            pltpu.VMEM((LEV, OBS), F32),
             pltpu.VMEM((OBS, COLS), BF16),
             pltpu.VMEM((1, OBS), F32),
+            pltpu.VMEM((LEV, 128), F32),
+            pltpu.VMEM((8 * LEV, COLS), F32),
+            pltpu.VMEM((LEV + 8, COLS), F32),
             pltpu.VMEM((LEV, COLS), F32),
-            pltpu.VMEM((8 * LEV, OBS), BF16),
-            pltpu.VMEM((8 * LEV, COLS), F32),
-            pltpu.VMEM((LEV, 512), F32),
-            pltpu.VMEM((LEV, COLS), F32),
-            pltpu.VMEM((ROWS, 64, 128), F32),
+            pltpu.VMEM((ROWS, 64, 128), BF16),
+            pltpu.VMEM((ROWS, 2, LEV, 128), F32),
+            pltpu.VMEM((ROWS, COLS), F32),
+            pltpu.VMEM((LEV, 128), F32),
             DMA((2, 4)),
             DMA((2, 3)),
+            DMA((4,)),
         ],
         compiler_params=pltpu.CompilerParams(
             vmem_limit_bytes=56 * 1024 * 1024, collective_id=1, has_side_effects=True
         ),
         name="column",
-    )(rows, meta, field, mixing, top, frac, thick, courant, shift, zfrac)
+    )(rows, meta, field.reshape(LEV, 64, 128), mixing, top, frac, thick, courant, shift, zfrac)
+
+
+def place(row, half):
+    return row // 8 * 16 + half * 8 + row % 8
 
 
 def transport_kernel(
-    conv_ref, halo_ref, next_conv_ref, next_halo_ref, next_given_ref,
-    shift_ref, frac_ref, courant_ref, out_ref, shift_pad, frac_pad, carried,
+    conv_hbm, halo_hbm, next_conv_ref, next_halo_ref, next_given_ref, shift_ref, courant_hbm, out_hbm,
+    conv, halo, courant, out, shifts, moved, conv_sems, courant_sems, halo_sems, out_sem,
 ):
-    step = pl.program_id(0)
-    lane = iota((LEV, 128), 1)
-    tail = jnp.where(iota((LEV, 128), 0) < 64, 0, PACK)
-
-    def zonal(first, second, packed, shift, fraction):
-        def pick(offset):
-            index = lane + offset
-            inside = index < 128
-            wrapped = index & 127
-            a = jnp.take_along_axis(first, wrapped, axis=1)
-            b = jnp.take_along_axis(second, wrapped, axis=1)
-            c = jnp.take_along_axis(packed, (wrapped + tail) & 127, axis=1)
-            return jnp.where(inside, a, b), jnp.where(inside, b, c)
-
-        left, right = pick(shift)
-        left_next, right_next = pick(shift + 1)
-        keep = 1.0 - fraction
-        return keep * left + fraction * left_next, keep * right + fraction * right_next
-
-    def doubled(packed):
-        return jnp.concatenate([packed, packed], axis=0)
-
-    @pl.when(step == 0)
-    def _():
-        rest = jnp.zeros((LEV - ROWS, 128), F32)
-        shifts = jnp.concatenate([shift_ref[...].astype(F32), rest], axis=0)
-        shift_pad[...] = jnp.transpose(shifts).astype(I32)
-        frac_pad[...] = jnp.transpose(jnp.concatenate([frac_ref[...], rest], axis=0))
-        last = lax.axis_index("lat") == NLAT - 1
-        shift = jnp.clip(next_given_ref[:, 256:384], 0.0, float(SHIFT_MAX)).astype(I32)
-        fraction = next_given_ref[:, 384:512]
-        left, right = zonal(
-            next_conv_ref[:, 0:128], next_conv_ref[:, 128:256], doubled(next_halo_ref[...]), shift, fraction
-        )
-        carried[:, 0:128] = jnp.where(last, 0.0, next_given_ref[:, 0:128] * left)
-        carried[:, 128:256] = jnp.where(last, 0.0, next_given_ref[:, 128:256] * right)
-
-    flat_courant = courant_ref.reshape(2048, 128)
-    flat_out = out_ref.reshape(2048, 128)
-    first_row = (3 - step) * 8
-
-    def row(back, carry):
-        r = 7 - back
-        here = jnp.full((LEV, 128), first_row + r, I32)
-        shift = jnp.take_along_axis(shift_pad[...], here, axis=1)
-        fraction = jnp.take_along_axis(frac_pad[...], here, axis=1)
-        parts = zonal(
-            conv_ref[r, :, 0:128], conv_ref[r, :, 128:256], doubled(halo_ref[r]), shift, fraction
-        )
+    last = lax.axis_index("lat") == NLAT - 1
+    groups = ROWS // GROUP
+
+    def conv_copy(group):
+        rows = pl.ds(group * GROUP, GROUP)
+        return pltpu.make_async_copy(conv_hbm.at[rows], conv.at[rows], conv_sems.at[group])
+
+    def halo_copy(group):
+        rows = pl.ds(group * GROUP, GROUP)
+        return pltpu.make_async_copy(halo_hbm.at[rows], halo.at[rows], halo_sems.at[group])
+
+    def fetch(group):
+        conv_copy(group).start()
+        halo_copy(group).start()
+        for i in range(GROUP):
+            row = group * GROUP + i
+            for half in range(2):
+                pltpu.make_async_copy(
+                    courant_hbm.at[:, place(row, half), :], courant.at[row, half], courant_sems.at[group]
+                ).start()
+
+    for ahead in range(AHEAD):
+        fetch(groups - 1 - ahead)
+
+    given = jnp.where(last, 0.0, next_given_ref[128:136, :])
+    blank = jnp.zeros((LEV - ROWS - 1, 128), F32)
+    shifts[...] = jnp.transpose(
+        jnp.concatenate([shift_ref[...].astype(F32), given[0:1, 0:128], blank], axis=0)
+    ).astype(I32)
+    lane = iota((PART, 128), 1)
+
+    def lanes(values, index):
+        return jnp.take_along_axis(values, index, axis=1, mode="promise_in_bounds")
+
+    def zonal(first, second, packed, part, row):
+        levels = pl.ds(part * PART, PART)
+        third = packed[pl.ds(part * PART % 64, PART), :].astype(F32)
+        if part * PART >= 64:
+            third = pltpu.roll(third, PACK, 1)
+        here = jnp.full((PART, 128), row, I32)
+        shift = lanes(shifts[levels, :], here)
+        second = second + jnp.where(lane == 127, third, 0.0)
+        index = lane + shift
+        wrapped = index & 127
+        a = lanes(jnp.where(lane < shift, third, first), wrapped)
+        b = lanes(second, wrapped)
+        inside = index < 128
+        return jnp.where(inside, a, b), jnp.where(inside, b, a)
+
+    for part in range(LEV // PART):
+        levels = pl.ds(part * PART, PART)
+        both = zonal(next_conv_ref[levels, 0:128], next_conv_ref[levels, 128:256], next_halo_ref, part, ROWS)
         for half in range(2):
-            at = pl.ds(half * 8 + r, 128, stride=16)
             span = pl.ds(half * 128, 128)
-            moved = flat_courant[at, :] * parts[half]
-            flat_out[at, :] = parts[half] - moved + carried[:, span]
-            carried[:, span] = moved
+            moved[half, levels, :] = jnp.where(last, 0.0, next_given_ref[levels, span] * both[half])
+    def step(back, carry):
+        group = groups - 1 - back
+        rows = pl.ds(group * GROUP, GROUP)
+
+        @pl.when(group >= AHEAD)
+        def _():
+            fetch(group - AHEAD)
+
+        conv_copy(group).wait()
+        halo_copy(group).wait()
+        pltpu.make_async_copy(courant.at[rows], courant.at[rows], courant_sems.at[group]).wait()
+        for part in range(LEV // PART):
+            levels = pl.ds(part * PART, PART)
+            coming = [moved[0, levels, :], moved[1, levels, :]]
+            for i in reversed(range(GROUP)):
+                row = group * GROUP + i
+                both = zonal(conv[row, levels, 0:128], conv[row, levels, 128:256], halo.at[row], part, row)
+                for half in range(2):
+                    leaving = courant[row, half, levels, :] * both[half]
+                    out[row, half, levels, :] = both[half] - leaving + coming[half]
+                    coming[half] = leaving
+            for half in range(2):
+                moved[half, levels, :] = coming[half]
+        for i in range(GROUP):
+            row = group * GROUP + i
+            for half in range(2):
+                pltpu.make_async_copy(
+                    out.at[row, half], out_hbm.at[:, place(row, half), :], out_sem
+                ).start()
         return carry
 
-    lax.fori_loop(0, 8, row, 0)
-
-
-def transport(conv, halo, next_conv, next_halo, next_given, shift, frac, courant):
-    whole = lambda *shape: pl.BlockSpec(shape, lambda i: (0,) * len(shape))
-    blocked = pl.BlockSpec((LEV, 1, 16, 128), lambda i: (0, 3 - i, 0, 0))
+    lax.fori_loop(0, groups, step, 0)
+    pltpu.make_async_copy(out, out, out_sem).wait()
+
+
+def transport(conv, halo, next_conv, next_halo, next_given, shift, courant):
+    vmem = pl.BlockSpec(memory_space=pltpu.VMEM)
+    anywhere = pl.BlockSpec(memory_space=pl.ANY)
     return pl.pallas_call(
         transport_kernel,
-        grid=(4,),
-        out_shape=jax.ShapeDtypeStruct((LEV, 4, 16, 128), F32),
-        in_specs=[
-            pl.BlockSpec((8, LEV, COLS), lambda i: (3 - i, 0, 0)),
-            pl.BlockSpec((8, 64, 128), lambda i: (3 - i, 0, 0)),
-            whole(LEV, COLS),
-            whole(64, 128),
-            whole(LEV, 512),
-            whole(ROWS, LEV),
-            whole(ROWS, LEV),
-            blocked,
-        ],
-        out_specs=blocked,
+        out_shape=jax.ShapeDtypeStruct((LEV, 64, 128), F32),
+        in_specs=[anywhere, anywhere] + [vmem] * 4 + [anywhere],
+        out_specs=anywhere,
         scratch_shapes=[
+            pltpu.VMEM((ROWS, LEV, COLS), F32),
+            pltpu.VMEM((ROWS, 64, 128), BF16),
+            pltpu.VMEM((ROWS, 2, LEV, 128), F32),
+            pltpu.VMEM((ROWS, 2, LEV, 128), F32),
             pltpu.VMEM((LEV, 128), I32),
-            pltpu.VMEM((LEV, 128), F32),
-            pltpu.VMEM((LEV, COLS), F32),
+            pltpu.VMEM((2, LEV, 128), F32),
+            DMA((ROWS // GROUP,)),
+            DMA((ROWS // GROUP,)),
+            DMA((ROWS // GROUP,)),
+            DMA,
         ],
         compiler_params=pltpu.CompilerParams(vmem_limit_bytes=60 * 1024 * 1024),
         name="transport",
-    )(conv, halo, next_conv, next_halo, next_given, shift, frac, courant)
+    )(conv, halo, next_conv, next_halo, next_given, shift, courant.reshape(LEV, 64, 128))
 
 
 def tiles(value):
@@ -429,7 +489,7 @@
         rows.reshape(OBS, LEV), meta.reshape(NDEV, 128), tiles(adjoint_field), mixing_inverse,
         cloud_top, conv_frac, thickness.reshape(1, LEV), courant, shift, zfrac,
     )
-    out = transport(conv, halo, next_conv, next_halo, next_given, shift, zfrac, courant)
+    out = transport(conv, halo, next_conv, next_halo, next_given, shift, courant)
     return untiles(out)
 
 

time: 68.3 us -> 54.3 us (0.80)
  Pallas kernels: 67.3 us -> 53.2 us
    pallas_call x1, Pallas kernels: 17.4 us -> 10.2 us  [transport(): pl.pallas_call(transport_kernel, out_shape=jax.ShapeDtypeStruct((LEV, 64,...]
    pallas_call x1, Pallas kernels: 30 us -> 23.1 us  [column_step(): pl.pallas_call(column_kernel, grid=(4,), out_shape=[jax.ShapeDtypeStruct(...]
where the time goes in v2:
time: 54.3 us; the launch traced here: 53.8 us
  Pallas kernels  53.2 us (98%)
  between operations  0.67 us (1%)
    pallas_call x1, Pallas kernels, column_step(): pl.pallas_call(column_kernel, grid=(4,), out_shape=[jax.ShapeDtypeStruct(...  23.1 us
    pallas_call x1, Pallas kernels, exchange(): pl.pallas_call(exchange_kernel, out_shape=[jax.ShapeDtypeStruct((NDEV, CA...  19.8 us
    pallas_call x1, Pallas kernels, transport(): pl.pallas_call(transport_kernel, out_shape=jax.ShapeDtypeStruct((LEV, 64,...  10.2 us

profile of v2, /device:TPU:15, one launch (start us, length us, event | category | flops | bytes accessed | tf_op | source)
XLA Modules:
  0.0 53.8 jit_solution(11662075796900304193)
XLA Ops:
  0.7 19.8 %exchange.1 = (bf16[128,16,128]{2,1,0:T(8,128)(2,1)}, s32[128,1,128]{2,1,0:T(1,128)}) custom-call(s32[1]{0:T(128)S(6)} %copy.14.count_ref, bf16[2048,128]{1,0:T(8,128)(2,1)} %kernel_ref.1, f32[16,128]{1,0:T(8,128)} %bitcast.33, s32[16,128]{1,0:T(8,128)} %bitcast.34, s32[16,128]{1,0:T(8,128)} %bitcast.35), custom_call_target="tpu_custom_call" | custom-call | tf_op jit(solution)/shard_map/exchange/pallas_call | solution.py:129
  20.5 23.1 %column.1 = (f32[32,128,256]{2,1,0:T(8,128)}, bf16[32,64,128]{2,1,0:T(8,128)(2,1)}, f32[128,256]{1,0:T(8,128)}, bf16[64,128]{1,0:T(8,128)(2,1)}, f32[136,256]{1,0:T(8,128)}) custom-call(bf16[2048,128]{1,0:T(8,128)(2,1)} %bitcast.28, s32[128,128]{1,0:T(8,128)} %bitcast.29, f32[128,64,128]{2,1,0:T(8,128)} %bitcast.27, f32[32,128,128]{2,1,0:T(8,128)} %mixing_ref.1, ...), custom_call_target="tpu_custom_call" | custom-call | tf_op jit(solution)/shard_map/column/pallas_call | solution.py:304
  43.6 10.2 %transport.1 = f32[128,64,128]{2,1,0:T(8,128)} custom-call(f32[32,128,256]{2,1,0:T(8,128)} %get-tuple-element.14.conv_hbm, bf16[32,64,128]{2,1,0:T(8,128)(2,1)} %get-tuple-element.15.halo_hbm, f32[128,256]{1,0:T(8,128)} %get-tuple-element.16.next_conv_ref, bf16[64,128]{1,0:T(8,128)(2,1)} %get-tuple-element.17.next_halo_ref, ...), custom_call_target="tpu_custom_call" | custom-call | tf_op jit(solution)/shard_map/transport/pallas_call | solution.py:451

commit v3 on v2

--- a/solution.py
+++ b/solution.py
@@ -16,7 +16,7 @@
 LEV, ROWS, COLS = 128, 32, 256
 OBS, CAP = 2048, 16
 PACK = 64
-PART = 32
+PART = 16
 GROUP = 2
 AHEAD = 4
 UNROLL = 4
@@ -69,7 +69,7 @@
         ).astype(BF16)
 
     pl.semaphore_wait(barrier, NLON + NLAT - 2)
-    greet(lat_peer, entered, NLAT)
+    greet(lat_peer, entered.at[lat], NLAT)
 
     big_sub = iota((128, 128), 0)
     mine = (big_sub // CAP) == lax.rem(me, 8)
@@ -86,31 +86,41 @@
     for dst in range(NDEV):
         send_meta[dst, :, :] = meta[dst : dst + 1, :]
 
+    slots = jnp.concatenate([slot[block : block + 1, :] for block in range(16)], axis=1)
     for out_block in range(16):
-        total = jnp.zeros((128, 128), F32)
-        for block in range(out_block + 1):
-            hit = jnp.where(slot[block : block + 1, :] == big_sub + out_block * 128, 1.0, 0.0).astype(BF16)
-            total = total + jnp.dot(
-                hit, contribution[pl.ds(block * 128, 128), :], preferred_element_type=F32
-            )
+        width = (out_block + 1) * 128
+        hit = jnp.where(slots[:, 0:width] - out_block * 128 == iota((128, width), 0), 1.0, 0.0).astype(BF16)
+        total = jnp.dot(hit, contribution[0:width, :], preferred_element_type=F32)
         send_rows[pl.ds(out_block * 8, 8), :, :] = total.astype(BF16).reshape(8, CAP, LEV)
 
-    pl.semaphore_wait(entered, NLAT - 1)
-
-    def send(step, carry):
-        target = lax.rem(me + step, NDEV)
-        where = (target // NLON, lax.rem(target, NLON))
+    def send_to(to_lat, to_lon):
+        target = to_lat * NLON + to_lon
         pltpu.make_async_remote_copy(
             send_rows.at[target], rows_out.at[me], sems.at[0], sems.at[1],
-            device_id=where, device_id_type=MESH,
+            device_id=(to_lat, to_lon), device_id_type=MESH,
         ).start()
         pltpu.make_async_remote_copy(
             send_meta.at[target], meta_out.at[me], sems.at[2], sems.at[3],
-            device_id=where, device_id_type=MESH,
+            device_id=(to_lat, to_lon), device_id_type=MESH,
         ).start()
+
+    def send_near(step, carry):
+        send_to(lat, lax.rem(lon + step, NLON))
         return carry
 
-    lax.fori_loop(1, NDEV, send, 0)
+    lax.fori_loop(1, NLON, send_near, 0)
+
+    def send_row(step, carry):
+        to_lat = lax.rem(lat + step, NLAT)
+        pl.semaphore_wait(entered.at[to_lat], 1)
+
+        def send_far(turn, inner):
+            send_to(to_lat, lax.rem(lon + turn, NLON))
+            return inner
+
+        return lax.fori_loop(0, NLON, send_far, carry)
+
+    lax.fori_loop(1, NLAT, send_row, 0)
     own_rows = pltpu.make_async_copy(send_rows.at[me], rows_out.at[me], sems.at[4])
     own_meta = pltpu.make_async_copy(send_meta.at[me], meta_out.at[me], sems.at[5])
     own_rows.start()
@@ -138,7 +148,7 @@
             pltpu.VMEM((NDEV, CAP, LEV), BF16),
             pltpu.VMEM((NDEV, 1, 128), I32),
             pltpu.VMEM((OBS, LEV), BF16),
-            pltpu.SemaphoreType.REGULAR,
+            pltpu.SemaphoreType.REGULAR((NLAT,)),
             DMA((6,)),
         ],
         compiler_params=pltpu.CompilerParams(collective_id=0, has_side_effects=True),
@@ -150,10 +160,10 @@
 
 
 def column_kernel(
-    rows_ref, meta_ref, field_hbm, mixing_ref, top_ref, frac_ref, thick_ref, courant_ref, shift_ref, zfrac_ref,
+    rows_ref, meta_ref, field_hbm, mixing_ref, top_ref, frac_ref, thick_ref, courant_hbm, shift_ref, zfrac_ref,
     out_ref, halo_in, next_in, next_halo_in, next_given_in,
     rows_t, cols_hot, row_of, thick_full, forced, given, first, edge, field, mass, weights, halo_sems, next_sems,
-    field_sems,
+    field_sems, courant_sems,
 ):
     step = pl.program_id(0)
     lat, lon = lax.axis_index("lat"), lax.axis_index("lon")
@@ -164,7 +174,7 @@
 
     def halo_copy(block):
         return pltpu.make_async_remote_copy(
-            edge.at[pl.ds(block * 8, 8)], halo_in.at[pl.ds(block * 8, 8)],
+            edge.at[pl.ds(block * 4, 4)], halo_in.at[pl.ds(block * 4, 4)],
             halo_sems.at[0, block], halo_sems.at[1, block], device_id=(lat, west), device_id_type=MESH,
         )
 
@@ -193,9 +203,16 @@
             (lat, west), (lat, east), (north, lon), (south, lon), (north, west), (south, east)
         ):
             pl.semaphore_signal(barrier, inc=1, device_id=target, device_id_type=MESH)
-        flat_courant = courant_ref.reshape(2048, 128)
-        given[0:128, 0:128] = flat_courant[pl.ds(0, 128, stride=16), :]
-        given[0:128, 128:256] = flat_courant[pl.ds(8, 128, stride=16), :]
+        first_courant = [
+            pltpu.make_async_copy(
+                courant_hbm.at[:, place(0, half), :],
+                given.at[pl.ds(0, LEV), pl.ds(half * 128, 128)],
+                courant_sems.at[half],
+            )
+            for half in range(2)
+        ]
+        for copy in first_courant:
+            copy.start()
         given[128:136, 0:128] = shift_ref[0:8, :].astype(F32)
         given[128:136, 128:256] = jnp.zeros((8, 128), F32)
         blank = jnp.zeros((LEV - ROWS, 128), F32)
@@ -222,6 +239,8 @@
             span = pl.ds(half * 128, 128)
             mass[:, span] = jnp.take_along_axis(sums, top_ref[:, span] - 1, axis=1, mode="promise_in_bounds")
         pl.semaphore_wait(barrier, 6)
+        for copy in first_courant:
+            copy.wait()
 
         @pl.when(has_north)
         def _():
@@ -271,10 +290,10 @@
     def rows_of(pair, carry):
         for i in range(UNROLL):
             one_row(pair * UNROLL + i)
+        halo_copy(step * 2 + pair).start()
         return carry
 
     lax.fori_loop(0, 8 // UNROLL, rows_of, 0)
-    halo_copy(step).start()
 
     @pl.when((step == 0) & has_north)
     def _():
@@ -294,7 +313,7 @@
             for which in range(3):
                 next_copy(which).wait_recv()
 
-        for block in range(4):
+        for block in range(ROWS // 4):
             halo_copy(block).wait()
 
 
@@ -319,7 +338,7 @@
             whole(ROWS, COLS),
             whole(ROWS, COLS),
             whole(1, LEV),
-            pl.BlockSpec((LEV, 1, 16, 128), lambda i: (0, 0, 0, 0)),
+            anywhere,
             whole(ROWS, LEV),
             whole(ROWS, LEV),
         ],
@@ -336,15 +355,16 @@
             pltpu.VMEM((ROWS, 2, LEV, 128), F32),
             pltpu.VMEM((ROWS, COLS), F32),
             pltpu.VMEM((LEV, 128), F32),
-            DMA((2, 4)),
+            DMA((2, ROWS // 4)),
             DMA((2, 3)),
             DMA((4,)),
+            DMA((2,)),
         ],
         compiler_params=pltpu.CompilerParams(
             vmem_limit_bytes=56 * 1024 * 1024, collective_id=1, has_side_effects=True
         ),
         name="column",
-    )(rows, meta, field.reshape(LEV, 64, 128), mixing, top, frac, thick, courant, shift, zfrac)
+    )(rows, meta, field.reshape(LEV, 64, 128), mixing, top, frac, thick, courant.reshape(LEV, 64, 128), shift, zfrac)
 
 
 def place(row, half):
@@ -381,9 +401,14 @@
 
     given = jnp.where(last, 0.0, next_given_ref[128:136, :])
     blank = jnp.zeros((LEV - ROWS - 1, 128), F32)
-    shifts[...] = jnp.transpose(
+    by_row = jnp.transpose(
         jnp.concatenate([shift_ref[...].astype(F32), given[0:1, 0:128], blank], axis=0)
-    ).astype(I32)
+    )
+    column = iota((LEV, 128), 1)
+    ones = jnp.ones((128, 128), BF16)
+    for row in range(ROWS + 1):
+        alone = jnp.where(column == row, by_row, 0.0).astype(BF16)
+        shifts[row, :, :] = jnp.dot(alone, ones, preferred_element_type=F32).astype(I32)
     lane = iota((PART, 128), 1)
 
     def lanes(values, index):
@@ -394,8 +419,7 @@
         third = packed[pl.ds(part * PART % 64, PART), :].astype(F32)
         if part * PART >= 64:
             third = pltpu.roll(third, PACK, 1)
-        here = jnp.full((PART, 128), row, I32)
-        shift = lanes(shifts[levels, :], here)
+        shift = shifts[row, levels, :]
         second = second + jnp.where(lane == 127, third, 0.0)
         index = lane + shift
         wrapped = index & 127
@@ -458,7 +482,7 @@
             pltpu.VMEM((ROWS, 64, 128), BF16),
             pltpu.VMEM((ROWS, 2, LEV, 128), F32),
             pltpu.VMEM((ROWS, 2, LEV, 128), F32),
-            pltpu.VMEM((LEV, 128), I32),
+            pltpu.VMEM((ROWS + 1, LEV, 128), I32),
             pltpu.VMEM((2, LEV, 128), F32),
             DMA((ROWS // GROUP,)),
             DMA((ROWS // GROUP,)),

time: 54.3 us -> 51.7 us (0.952)
  Pallas kernels: 53.2 us -> 50.6 us
    pallas_call x1, Pallas kernels: 23.1 us -> 21 us  [column_step(): pl.pallas_call(column_kernel, grid=(4,), out_shape=[jax.ShapeDtypeStruct(...]
    pallas_call x1, Pallas kernels: 10.2 us -> 9.04 us  [transport(): pl.pallas_call(transport_kernel, out_shape=jax.ShapeDtypeStruct((LEV, 64,...]
    pallas_call x1, Pallas kernels: 19.8 us -> 20.6 us  [exchange(): pl.pallas_call(exchange_kernel, out_shape=[jax.ShapeDtypeStruct((NDEV, CA...]
where the time goes in v3:
time: 51.7 us; the launch traced here: 51.3 us
  Pallas kernels  50.6 us (98%)
  between operations  0.67 us (1%)
    pallas_call x1, Pallas kernels, column_step(): pl.pallas_call(column_kernel, grid=(4,), out_shape=[jax.ShapeDtypeStruct(...  21 us
    pallas_call x1, Pallas kernels, exchange(): pl.pallas_call(exchange_kernel, out_shape=[jax.ShapeDtypeStruct((NDEV, CA...  20.6 us
    pallas_call x1, Pallas kernels, transport(): pl.pallas_call(transport_kernel, out_shape=jax.ShapeDtypeStruct((LEV, 64,...  9.04 us

profile of v3, /device:TPU:15, one launch (start us, length us, event | category | flops | bytes accessed | tf_op | source)
XLA Modules:
  0.0 51.3 jit_solution(12051223789138864030)
XLA Ops:
  0.7 20.6 %exchange.1 = (bf16[128,16,128]{2,1,0:T(8,128)(2,1)}, s32[128,1,128]{2,1,0:T(1,128)}) custom-call(s32[1]{0:T(128)S(6)} %copy.14.count_ref, bf16[2048,128]{1,0:T(8,128)(2,1)} %kernel_ref.1, f32[16,128]{1,0:T(8,128)} %bitcast.31, s32[16,128]{1,0:T(8,128)} %bitcast.32, s32[16,128]{1,0:T(8,128)} %bitcast.33), custom_call_target="tpu_custom_call" | custom-call | tf_op jit(solution)/shard_map/exchange/pallas_call | solution.py:139
  21.2 21.0 %column.1 = (f32[32,128,256]{2,1,0:T(8,128)}, bf16[32,64,128]{2,1,0:T(8,128)(2,1)}, f32[128,256]{1,0:T(8,128)}, bf16[64,128]{1,0:T(8,128)(2,1)}, f32[136,256]{1,0:T(8,128)}) custom-call(bf16[2048,128]{1,0:T(8,128)(2,1)} %bitcast.26, s32[128,128]{1,0:T(8,128)} %bitcast.27, f32[128,64,128]{2,1,0:T(8,128)} %bitcast.25, f32[32,128,128]{2,1,0:T(8,128)} %mixing_ref.1, ...), custom_call_target="tpu_custom_call" | custom-call | tf_op jit(solution)/shard_map/column/pallas_call | solution.py:323
  42.2 9.0 %transport.1 = f32[128,64,128]{2,1,0:T(8,128)} custom-call(f32[32,128,256]{2,1,0:T(8,128)} %get-tuple-element.14.conv_hbm, bf16[32,64,128]{2,1,0:T(8,128)(2,1)} %get-tuple-element.15.halo_hbm, f32[128,256]{1,0:T(8,128)} %get-tuple-element.16.next_conv_ref, bf16[64,128]{1,0:T(8,128)(2,1)} %get-tuple-element.17.next_halo_ref, ...), custom_call_target="tpu_custom_call" | custom-call | tf_op jit(solution)/shard_map/transport/pallas_call | solution.py:475

commit v4 on v3

--- a/solution.py
+++ b/solution.py
@@ -61,12 +61,18 @@
     cell_row = (cells // COLS).astype(F32)
     cell_col = (cells % COLS).astype(F32)
 
-    depart_t = jnp.transpose(depart_ref[...])
+    exact = depart_ref[...]
+    high = exact.astype(BF16).astype(F32)
+    middle = (exact - high).astype(BF16).astype(F32)
+    thirds = [high, middle, exact - high - middle, jnp.zeros((80, 128), F32)]
+    depart_t = jnp.transpose(jnp.concatenate(thirds, axis=0))
+    place_of = iota((128, 128), 1) % 16
+    every = jnp.ones((128, 128), BF16)
     for block in range(16):
         span = pl.ds(block * 128, 128)
-        contribution[span, :] = (
-            kernel_ref[span, :].astype(F32) * jnp.broadcast_to(depart_t[:, block : block + 1], (128, 128))
-        ).astype(BF16)
+        alone = jnp.where(place_of == block, depart_t, 0.0).astype(BF16)
+        spread = jnp.dot(alone, every, preferred_element_type=F32)
+        contribution[span, :] = (kernel_ref[span, :].astype(F32) * spread).astype(BF16)
 
     pl.semaphore_wait(barrier, NLON + NLAT - 2)
     greet(lat_peer, entered.at[lat], NLAT)
@@ -86,11 +92,14 @@
     for dst in range(NDEV):
         send_meta[dst, :, :] = meta[dst : dst + 1, :]
 
-    slots = jnp.concatenate([slot[block : block + 1, :] for block in range(16)], axis=1)
     for out_block in range(16):
         width = (out_block + 1) * 128
-        hit = jnp.where(slots[:, 0:width] - out_block * 128 == iota((128, width), 0), 1.0, 0.0).astype(BF16)
-        total = jnp.dot(hit, contribution[0:width, :], preferred_element_type=F32)
+        wanted = big_sub + out_block * 128
+        hits = [
+            jnp.where(slot[block : block + 1, :] == wanted, 1.0, 0.0).astype(BF16)
+            for block in range(out_block + 1)
+        ]
+        total = jnp.dot(jnp.concatenate(hits, axis=1), contribution[0:width, :], preferred_element_type=F32)
         send_rows[pl.ds(out_block * 8, 8), :, :] = total.astype(BF16).reshape(8, CAP, LEV)
 
     def send_to(to_lat, to_lon):
@@ -108,7 +117,7 @@
         send_to(lat, lax.rem(lon + step, NLON))
         return carry
 
-    lax.fori_loop(1, NLON, send_near, 0)
+    lax.fori_loop(1, NLON, send_near, 0, unroll=5)
 
     def send_row(step, carry):
         to_lat = lax.rem(lat + step, NLAT)
@@ -118,7 +127,7 @@
             send_to(to_lat, lax.rem(lon + turn, NLON))
             return inner
 
-        return lax.fori_loop(0, NLON, send_far, carry)
+        return lax.fori_loop(0, NLON, send_far, carry, unroll=8)
 
     lax.fori_loop(1, NLAT, send_row, 0)
     own_rows = pltpu.make_async_copy(send_rows.at[me], rows_out.at[me], sems.at[4])
@@ -222,12 +231,15 @@
         columns = jnp.transpose((cells % COLS).astype(F32))
         eye = jnp.where(iota((128, 128), 0) == iota((128, 128), 1), 1.0, 0.0).astype(BF16)
         wide = iota((128, COLS), 1).astype(F32)
+        columns = jnp.concatenate([columns, jnp.zeros((128, 112), F32)], axis=1)
+        place_lane = iota((128, 128), 1)
+        every = jnp.ones((128, COLS), BF16)
         for b in range(16):
             row_of[:, b * 128 : b * 128 + 128] = cell_rows[b : b + 1, :]
             span = pl.ds(b * 128, 128)
-            cols_hot[span, :] = jnp.where(
-                jnp.broadcast_to(columns[:, b : b + 1], (128, COLS)) == wide, 1.0, 0.0
-            ).astype(BF16)
+            alone = jnp.where(place_lane == b, columns, 0.0).astype(BF16)
+            spread = jnp.dot(alone, every, preferred_element_type=F32)
+            cols_hot[span, :] = jnp.where(spread == wide, 1.0, 0.0).astype(BF16)
             rows_t[:, span] = lax.dot_general(
                 eye, rows_ref[span, :], (((1,), (1,)), ((), ())), preferred_element_type=F32
             )

time: 51.7 us -> 51.7 us (level)
  no operation moved by 1% of the time
where the time goes in v4:
time: 51.7 us; the launch traced here: 51.1 us
  Pallas kernels  50.5 us (98%)
  between operations  0.67 us (1%)
    pallas_call x1, Pallas kernels, column_step(): pl.pallas_call(column_kernel, grid=(4,), out_shape=[jax.ShapeDtypeStruct(...  20.9 us
    pallas_call x1, Pallas kernels, exchange(): pl.pallas_call(exchange_kernel, out_shape=[jax.ShapeDtypeStruct((NDEV, CA...  20.6 us
    pallas_call x1, Pallas kernels, transport(): pl.pallas_call(transport_kernel, out_shape=jax.ShapeDtypeStruct((LEV, 64,...  9.04 us

profile of v4, /device:TPU:15, one launch (start us, length us, event | category | flops | bytes accessed | tf_op | source)
XLA Modules:
  0.0 51.1 jit_solution(6932517261475903699)
XLA Ops:
  0.7 20.6 %exchange.1 = (bf16[128,16,128]{2,1,0:T(8,128)(2,1)}, s32[128,1,128]{2,1,0:T(1,128)}) custom-call(s32[1]{0:T(128)S(6)} %copy.14.count_ref, bf16[2048,128]{1,0:T(8,128)(2,1)} %kernel_ref.1, f32[16,128]{1,0:T(8,128)} %bitcast.31, s32[16,128]{1,0:T(8,128)} %bitcast.32, s32[16,128]{1,0:T(8,128)} %bitcast.33), custom_call_target="tpu_custom_call" | custom-call | tf_op jit(solution)/shard_map/exchange/pallas_call | solution.py:148
  21.2 20.9 %column.1 = (f32[32,128,256]{2,1,0:T(8,128)}, bf16[32,64,128]{2,1,0:T(8,128)(2,1)}, f32[128,256]{1,0:T(8,128)}, bf16[64,128]{1,0:T(8,128)(2,1)}, f32[136,256]{1,0:T(8,128)}) custom-call(bf16[2048,128]{1,0:T(8,128)(2,1)} %bitcast.26, s32[128,128]{1,0:T(8,128)} %bitcast.27, f32[128,64,128]{2,1,0:T(8,128)} %bitcast.25, f32[32,128,128]{2,1,0:T(8,128)} %mixing_ref.1, ...), custom_call_target="tpu_custom_call" | custom-call | tf_op jit(solution)/shard_map/column/pallas_call | solution.py:335
  42.1 9.0 %transport.1 = f32[128,64,128]{2,1,0:T(8,128)} custom-call(f32[32,128,256]{2,1,0:T(8,128)} %get-tuple-element.14.conv_hbm, bf16[32,64,128]{2,1,0:T(8,128)(2,1)} %get-tuple-element.15.halo_hbm, f32[128,256]{1,0:T(8,128)} %get-tuple-element.16.next_conv_ref, bf16[64,128]{1,0:T(8,128)(2,1)} %get-tuple-element.17.next_halo_ref, ...), custom_call_target="tpu_custom_call" | custom-call | tf_op jit(solution)/shard_map/transport/pallas_call | solution.py:487

commit v5 on v4

--- a/solution.py
+++ b/solution.py
@@ -18,7 +18,7 @@
 PACK = 64
 PART = 16
 GROUP = 2
-AHEAD = 4
+AHEAD = 6
 UNROLL = 4
 
 

time: 51.7 us -> 51.8 us (level)
  no operation moved by 1% of the time
where the time goes in v5:
time: 51.8 us; the launch traced here: 51.3 us
  Pallas kernels  50.7 us (98%)
  between operations  0.67 us (1%)
    pallas_call x1, Pallas kernels, column_step(): pl.pallas_call(column_kernel, grid=(4,), out_shape=[jax.ShapeDtypeStruct(...  20.9 us
    pallas_call x1, Pallas kernels, exchange(): pl.pallas_call(exchange_kernel, out_shape=[jax.ShapeDtypeStruct((NDEV, CA...  20.6 us
    pallas_call x1, Pallas kernels, transport(): pl.pallas_call(transport_kernel, out_shape=jax.ShapeDtypeStruct((LEV, 64,...  9.24 us

profile of v5, /device:TPU:15, one launch (start us, length us, event | category | flops | bytes accessed | tf_op | source)
XLA Modules:
  0.0 51.3 jit_solution(7601667695337323665)
XLA Ops:
  0.7 20.6 %exchange.1 = (bf16[128,16,128]{2,1,0:T(8,128)(2,1)}, s32[128,1,128]{2,1,0:T(1,128)}) custom-call(s32[1]{0:T(128)S(6)} %copy.14.count_ref, bf16[2048,128]{1,0:T(8,128)(2,1)} %kernel_ref.1, f32[16,128]{1,0:T(8,128)} %bitcast.31, s32[16,128]{1,0:T(8,128)} %bitcast.32, s32[16,128]{1,0:T(8,128)} %bitcast.33), custom_call_target="tpu_custom_call" | custom-call | tf_op jit(solution)/shard_map/exchange/pallas_call | solution.py:148
  21.2 20.9 %column.1 = (f32[32,128,256]{2,1,0:T(8,128)}, bf16[32,64,128]{2,1,0:T(8,128)(2,1)}, f32[128,256]{1,0:T(8,128)}, bf16[64,128]{1,0:T(8,128)(2,1)}, f32[136,256]{1,0:T(8,128)}) custom-call(bf16[2048,128]{1,0:T(8,128)(2,1)} %bitcast.26, s32[128,128]{1,0:T(8,128)} %bitcast.27, f32[128,64,128]{2,1,0:T(8,128)} %bitcast.25, f32[32,128,128]{2,1,0:T(8,128)} %mixing_ref.1, ...), custom_call_target="tpu_custom_call" | custom-call | tf_op jit(solution)/shard_map/column/pallas_call | solution.py:335
  42.1 9.2 %transport.1 = f32[128,64,128]{2,1,0:T(8,128)} custom-call(f32[32,128,256]{2,1,0:T(8,128)} %get-tuple-element.14.conv_hbm, bf16[32,64,128]{2,1,0:T(8,128)(2,1)} %get-tuple-element.15.halo_hbm, f32[128,256]{1,0:T(8,128)} %get-tuple-element.16.next_conv_ref, bf16[64,128]{1,0:T(8,128)(2,1)} %get-tuple-element.17.next_halo_ref, ...), custom_call_target="tpu_custom_call" | custom-call | tf_op jit(solution)/shard_map/transport/pallas_call | solution.py:487
